TPU v7x, 256 devices: a whole 4x4x8 slice. The times are simulated.
256 devices in a mesh: fsdp: 2 (over y_hi), dp: 32 (over x, z), owner: 4 (over y_lo, core).
Axes of the slice: x: 4, y: 4 (y_hi: 2, y_lo: 2; y = y_hi * 2 + y_lo), z: 8, core: 2. Of those that a mesh axis runs over, the one named last changes fastest.
Arguments:
- hidden: bfloat16 [256, 256, 4096], P(('fsdp', 'dp', 'owner')), may hold values from -6 to 6
- norm_gain: float32 [4096], replicated, may hold values from 0.1 to 1.9
- query_weight: bfloat16 [4096, 2048], P(('fsdp', 'dp')), may hold values from -0.09375 to 0.09375
- key_value_weight: bfloat16 [4096, 1024], P(('fsdp', 'dp')), may hold values from -0.09375 to 0.09375
- lengths: int32 [256], P(('fsdp', 'dp', 'owner')), may hold values from 128 to 256, as said below
- cotangent: bfloat16 [256, 256, 2048], P(('fsdp', 'dp', 'owner')), may hold values from -6 to 6
- cartridge: float32 [512, 1024], P('owner'), may hold values from -48 to 48
- adam_first_moment: float32 [512, 1024], P('owner'), may hold values from -6 to 6
- adam_second_moment: float32 [512, 1024], P('owner'), may hold values from 0.01 to 1
Outputs:
- attention_out: bfloat16 [256, 256, 2048], P(('fsdp', 'dp', 'owner'))
- new_cartridge: float32 [512, 1024], P('owner')
- new_first: float32 [512, 1024], P('owner')
- new_second: float32 [512, 1024], P('owner')
Inputs may be any that keep to these rules, and one draw needn't show every extreme that they name: `lengths`: each conversation's live tokens are its first rows; the rows after them are padding; some conversation is full.
All inputs are finite; a program needn't handle non-finite values.
Results may differ from a plain program's by a relative error of at most 0.008.
The roundings to bfloat16 on the way count: a program that leaves them out, or rounds other values in their place, can miss the bound.
Values may be sent and summed in bfloat16 or wider, within the bound.
No kernel may reach another device: no remote copies, remote signals or barrier semaphores. Data moves between devices by JAX's collectives and lax.ppermute only.
A program may use at most 128 MiB of HBM per device.

v0:
```python
import jax
import jax.numpy as jnp
from jax import lax
from jax.experimental import pallas as pl
from jax.experimental.pallas import tpu as pltpu
from jax.sharding import PartitionSpec as P


HEAD_SIZE = 128
GROUP = 4
STEP = 50
ROWS = 256
WIDTH = 4096
PREFIX = 512
COLS = 768
HALF = 384
MESH_AXES = ("fsdp", "dp", "owner")
X_SIZE, Z_SIZE = 4, 8
LOG2E = 1.4426950408889634


def coords(i):
    return i // 128, (i % 128) // 32, (i // 4) % 8, (i // 2) % 2, i % 2


def device_at(y_hi, x, z, y_lo, core):
    return y_hi * 128 + (x * 8 + z) * 4 + y_lo * 2 + core


def permute(value, move):
    pairs = [(i, device_at(*move(*coords(i)))) for i in range(256)]
    return lax.ppermute(value, MESH_AXES, pairs)


def along_z(step):
    return lambda y_hi, x, z, y_lo, core: (y_hi, x, (z + step) % Z_SIZE, y_lo, core)


def along_x(step):
    return lambda y_hi, x, z, y_lo, core: (y_hi, (x + step) % X_SIZE, z, y_lo, core)


def other_core(y_hi, x, z, y_lo, core):
    return y_hi, x, z, y_lo, 1 - core


def pair_chip(y_hi, x, z, y_lo, core):
    return y_hi, x, z, 1 - y_lo, core


def across_y(y_hi, x, z, y_lo, core):
    return 1 - y_hi, x, z, 1 - y_lo, core


def other_pair(y_hi, x, z, y_lo, core):
    return y_hi, x, z, 1 - y_lo, 1 - core


OWNERS = (other_core, pair_chip, other_pair)
Z_GROUPS = [[x * Z_SIZE + z for z in range(Z_SIZE)] for x in range(X_SIZE)]


def spread(value, axes, members, groups=None):
    copies = jnp.broadcast_to(value[None], (members,) + value.shape)
    return lax.all_to_all(copies, axes, 0, 0, axis_index_groups=groups, tiled=True)


def rope_tables():
    exponent = jnp.arange(HEAD_SIZE // 2, dtype=jnp.float32) * (2.0 / HEAD_SIZE)
    inverse = jnp.power(jnp.float32(500000.0), -exponent)
    position = (PREFIX + jnp.arange(ROWS)).astype(jnp.float32)
    angles = position[:, None] * inverse[None, :]
    cosine, sine = jnp.cos(angles), jnp.sin(angles)
    return (
        jnp.concatenate([cosine, cosine], axis=1),
        jnp.concatenate([-sine, sine], axis=1),
    )


def dot(a, b, a_dim, b_dim):
    return lax.dot_general(
        a, b, (((a_dim,), (b_dim,)), ((), ())), preferred_element_type=jnp.float32
    )


def norm_kernel(states, gain, normed):
    wide = states[0].astype(jnp.float32)
    scale = lax.rsqrt(jnp.mean(wide * wide, axis=1, keepdims=True) + 1e-05)
    normed[...] = (wide * scale * gain[...]).astype(jnp.bfloat16)


def normalise(hidden, gain):
    return pl.pallas_call(
        norm_kernel,
        grid=(4,),
        in_specs=[
            pl.BlockSpec((1, 64, WIDTH), lambda i: (0, i, 0)),
            pl.BlockSpec((1, WIDTH), lambda i: (0, 0)),
        ],
        out_specs=pl.BlockSpec((64, WIDTH), lambda i: (i, 0)),
        out_shape=jax.ShapeDtypeStruct((ROWS, WIDTH), jnp.bfloat16),
    )(hidden, gain.reshape(1, WIDTH))


def live(length):
    return lax.broadcasted_iota(jnp.int32, (ROWS, 512), 0) < length


def pack_kernel(place, cotangent, key_rows, value_rows, *packed):
    for index in range(4):

        @pl.when(pl.program_id(0) == index)
        def _():
            target = packed[index]
            target[0:ROWS, :] = jnp.where(live(place[4]), cotangent[0], 0).astype(jnp.bfloat16)
            for half in range(2):
                rows = slice(half * 64, half * 64 + 64)
                target[ROWS:, half * 128 : half * 128 + 128] = key_rows[rows, :].astype(
                    jnp.bfloat16
                )
                target[ROWS:, 256 + half * 128 : 384 + half * 128] = value_rows[rows, :].astype(
                    jnp.bfloat16
                )


def pack(place, cotangent, cartridge):
    return pl.pallas_call(
        pack_kernel,
        grid_spec=pltpu.PrefetchScalarGridSpec(
            num_scalar_prefetch=1,
            grid=(4,),
            in_specs=[
                pl.BlockSpec((1, ROWS, 512), lambda i, place: (0, 0, place[0] ^ i)),
                pl.BlockSpec((128, 128), lambda i, place: (0, place[0] ^ i)),
                pl.BlockSpec((128, 128), lambda i, place: (0, 4 + (place[0] ^ i))),
            ],
            out_specs=[pl.BlockSpec((320, 512), lambda i, place: (0, 0))] * 4,
        ),
        out_shape=[jax.ShapeDtypeStruct((320, 512), jnp.bfloat16)] * 4,
    )(place, cotangent, cartridge, cartridge)


def unpack_kernel(place, *refs):
    out = refs[4]
    for index in range(4):

        @pl.when(pl.program_id(0) == index)
        def _():
            out[0] = jnp.where(live(place[4]), refs[index][...], 0).astype(jnp.bfloat16)


def unpack(place, pieces):
    return pl.pallas_call(
        unpack_kernel,
        grid_spec=pltpu.PrefetchScalarGridSpec(
            num_scalar_prefetch=1,
            grid=(4,),
            in_specs=[pl.BlockSpec((ROWS, 512), lambda i, place: (0, 0))] * 4,
            out_specs=pl.BlockSpec((1, ROWS, 512), lambda i, place: (0, 0, place[0] ^ i)),
        ),
        out_shape=jax.ShapeDtypeStruct((1, ROWS, 2048), jnp.bfloat16),
    )(place, *pieces)


def layer_kernel(place, *refs):
    states = refs[0:4]
    z_pieces = refs[4:12]
    x_pieces = refs[12:17]
    packed, cosine, sine = refs[17:21], refs[21], refs[22]
    outs, gradient = refs[23:27], refs[27]
    weights, rows, keys, values, ups, out, sums, piece_sem, row_sem, up_sem = refs[28:]
    step = pl.program_id(0)
    y_hi, x, z = place[1], place[2], place[3]

    def piece_copies():
        copies = []

        def add(source, target):
            copies.append(
                pltpu.make_async_copy(source, target, piece_sem.at[len(copies)])
            )

        offsets = (0, -1, 1, -2, 2, -3, 3, 4)
        for side in range(2):
            y_from = y_hi if side == 0 else 1 - y_hi
            part = pl.ds(side * 64, 64)
            for piece, offset in zip(z_pieces, offsets):
                z_from = lax.rem(z + (offset + Z_SIZE), Z_SIZE)
                for back in range(X_SIZE):
                    x_from = lax.rem(x + (X_SIZE - back), X_SIZE)
                    add(
                        piece.at[back, part, :],
                        weights.at[y_from, x_from, z_from, :, pl.ds(0, HALF)],
                    )
            for piece, offset in zip(x_pieces[:3], (0, -1, 1)):
                x_from = lax.rem(x + (offset + X_SIZE), X_SIZE)
                add(
                    piece.at[:, part, :],
                    weights.at[y_from, x_from, :, :, pl.ds(HALF, HALF)],
                )
            x_from = lax.rem(x + 2, X_SIZE)
            add(
                x_pieces[3].at[:, part, :],
                weights.at[y_from, x_from, pl.ds(0, 4), :, pl.ds(HALF, HALF)],
            )
            add(
                x_pieces[4].at[:, part, :],
                weights.at[y_from, x_from, pl.ds(4, 4), :, pl.ds(HALF, HALF)],
            )
        return copies

    def row_copy(index):
        slot = index % 2
        return pltpu.make_async_copy(states[index], rows.at[slot], row_sem.at[slot])

    def up_copies():
        return [
            pltpu.make_async_copy(packed[index], ups.at[index], up_sem.at[index])
            for index in range(4)
        ]

    @pl.when(step == 0)
    def _():
        for copy in piece_copies():
            copy.start()
        row_copy(0).start()
        row_copy(1).start()
        for copy in up_copies():
            copy.start()
        sums[...] = jnp.zeros_like(sums)
        for copy in up_copies():
            copy.wait()
        for index in range(4):
            first = pl.multiple_of((place[0] ^ index) * 128, 128)
            for half in range(2):
                target = pl.ds(first + half * 64, 64)
                keys[target, :] = ups[index, ROWS:, half * 128 : half * 128 + 128]
                values[target, :] = ups[index, ROWS:, 256 + half * 128 : 384 + half * 128]
        for copy in piece_copies():
            copy.wait()

    for index in range(4):

        @pl.when(step == index)
        def _():
            if index in (1, 2):
                row_copy(index + 1).start()
            row_copy(index).wait()

    slot = lax.rem(step, 2)
    projected = dot(rows[slot], weights[...].reshape(WIDTH, COLS), 1, 0)
    cos, sin = cosine[...], sine[...]

    def rope(v):
        return (v * cos + pltpu.roll(v, HEAD_SIZE // 2, 1) * sin).astype(jnp.bfloat16)

    own_keys = rope(projected[:, 512:640])
    own_values = projected[:, 640:768].astype(jnp.bfloat16)
    prefix_keys, prefix_values = keys[...], values[...]
    causal = lax.broadcasted_iota(jnp.int32, (ROWS, ROWS), 0) >= lax.broadcasted_iota(
        jnp.int32, (ROWS, ROWS), 1
    )
    scale = HEAD_SIZE ** (-0.5) * LOG2E
    key_sum = jnp.zeros((HEAD_SIZE, PREFIX), jnp.float32)
    value_sum = jnp.zeros((HEAD_SIZE, PREFIX), jnp.float32)
    for head in range(GROUP):
        lanes = slice(head * HEAD_SIZE, (head + 1) * HEAD_SIZE)
        query = rope(projected[:, lanes])
        upstream = ups[step, 0:ROWS, lanes]
        before = dot(query, prefix_keys, 1, 1) * scale
        own = jnp.where(causal, dot(query, own_keys, 1, 1) * scale, -1e30)
        highest = jnp.maximum(
            jnp.max(before, axis=1, keepdims=True), jnp.max(own, axis=1, keepdims=True)
        )
        before = jnp.exp2(before - highest)
        own = jnp.exp2(own - highest)
        total = jnp.sum(before, axis=1, keepdims=True) + jnp.sum(own, axis=1, keepdims=True)
        inverse = 1.0 / total
        probs = before * inverse
        probs_low = probs.astype(jnp.bfloat16)
        own_low = (own * inverse).astype(jnp.bfloat16)
        attended = (
            dot(probs_low, prefix_values, 1, 0) + dot(own_low, own_values, 1, 0)
        ).astype(jnp.bfloat16)
        out[:, lanes] = attended
        delta = jnp.sum(
            upstream.astype(jnp.float32) * attended.astype(jnp.float32),
            axis=1,
            keepdims=True,
        )
        dprob = dot(upstream, prefix_values, 1, 1)
        dscore = (probs * (dprob - delta)).astype(jnp.bfloat16)
        key_sum += dot(query, dscore, 0, 0)
        value_sum += dot(upstream, probs_low, 0, 0)
    sums[0:HEAD_SIZE, :] += key_sum * HEAD_SIZE ** (-0.5)
    sums[HEAD_SIZE:, :] += value_sum

    for index in range(4):

        @pl.when(step == index)
        def _():
            outs[index][...] = out[...]

    @pl.when(step == 3)
    def _():
        gradient[...] = sums[...].T.astype(gradient.dtype)


def layer(place, states, z_pieces, x_pieces, packed, cosine, sine):
    anywhere = pl.BlockSpec(memory_space=pl.ANY)

    def whole(shape):
        return pl.BlockSpec(
            shape, lambda i, place: (0,) * len(shape), pipeline_mode=pl.Buffered(1)
        )

    return pl.pallas_call(
        layer_kernel,
        grid_spec=pltpu.PrefetchScalarGridSpec(
            num_scalar_prefetch=1,
            grid=(4,),
            in_specs=[anywhere] * 21 + [whole(cosine.shape), whole(sine.shape)],
            out_specs=[pl.BlockSpec((ROWS, 512), lambda i, place: (0, 0))] * 4
            + [
                pl.BlockSpec((PREFIX, 256), lambda i, place: (0, 0)),
            ],
            scratch_shapes=[
                pltpu.VMEM((2, X_SIZE, Z_SIZE, 64, COLS), jnp.bfloat16),
                pltpu.VMEM((2, ROWS, WIDTH), jnp.bfloat16),
                pltpu.VMEM((PREFIX, HEAD_SIZE), jnp.bfloat16),
                pltpu.VMEM((PREFIX, HEAD_SIZE), jnp.bfloat16),
                pltpu.VMEM((4, 320, 512), jnp.bfloat16),
                pltpu.VMEM((ROWS, 512), jnp.bfloat16),
                pltpu.VMEM((256, PREFIX), jnp.float32),
                pltpu.SemaphoreType.DMA((74,)),
                pltpu.SemaphoreType.DMA((2,)),
                pltpu.SemaphoreType.DMA((4,)),
            ],
        ),
        out_shape=[jax.ShapeDtypeStruct((ROWS, 512), jnp.bfloat16)] * 4
        + [
            jax.ShapeDtypeStruct((PREFIX, 256), jnp.bfloat16),
        ],
        compiler_params=pltpu.CompilerParams(dimension_semantics=("arbitrary",)),
    )(place, *states, *z_pieces, *x_pieces, *packed, cosine, sine)


def of_head(query_weight, key_value_weight, index):
    return jnp.concatenate(
        [
            lax.dynamic_slice_in_dim(query_weight, index * 512, 512, 1),
            lax.dynamic_slice_in_dim(key_value_weight, index * 128, 128, 1),
            lax.dynamic_slice_in_dim(key_value_weight, 512 + index * 128, 128, 1),
        ],
        axis=1,
    )


def gather_weights(own, across):
    both = jnp.concatenate([own, across], axis=0)
    first = both[:, :HALF]
    first = jnp.stack([first] + [permute(first, along_x(step)) for step in (1, 2, 3)])
    second = spread(both[:, HALF:], "dp", Z_SIZE, Z_GROUPS)
    z_pieces = [first]
    up, down = first, first
    for _ in range(3):
        up, down = permute(up, along_z(1)), permute(down, along_z(-1))
        z_pieces += [up, down]
    z_pieces += [permute(up, along_z(1))]
    up, down = permute(second, along_x(1)), permute(second, along_x(-1))
    x_pieces = [second, up, down]
    x_pieces += [permute(up[:4], along_x(1)), permute(down[4:], along_x(-1))]
    return z_pieces, x_pieces


def adam_update(current, moment_one, moment_two, prefix_gradient):
    one_new = 0.9 * moment_one + 0.1 * prefix_gradient
    two_new = 0.999 * moment_two + 0.001 * prefix_gradient * prefix_gradient
    one_fix = 1.0 - 0.9**STEP
    two_fix = 1.0 - 0.999**STEP
    updated = current - 0.02 * (one_new / one_fix) / (jnp.sqrt(two_new / two_fix) + 1e-08)
    return (updated, one_new, two_new)


def layer_step(
    hidden,
    norm_gain,
    query_weight,
    key_value_weight,
    lengths,
    cotangent,
    cartridge,
    adam_first_moment,
    adam_second_moment,
):
    head = lax.axis_index("owner")
    replica = lax.axis_index("dp")
    cosine, sine = rope_tables()
    place = jnp.stack(
        [head, lax.axis_index("fsdp"), replica // Z_SIZE, replica % Z_SIZE, lengths[0]]
    ).astype(jnp.int32)
    sent = of_head(query_weight, key_value_weight, head ^ 2)
    own = of_head(query_weight, key_value_weight, head)
    own, sent, hidden = lax.optimization_barrier((own, sent, hidden))
    across = permute(sent, across_y)
    normed = normalise(hidden, norm_gain)
    far = permute(normed, pair_chip)
    near = permute(normed, other_core)
    packed = pack(place, cotangent, cartridge)
    across, packed, cosine, sine = lax.optimization_barrier((across, packed, cosine, sine))
    z_pieces, x_pieces = gather_weights(own, across)
    packed = [packed[0]] + [permute(v, m) for v, m in zip(packed[1:], OWNERS)]
    far, z_pieces[5], z_pieces[6] = lax.optimization_barrier((far, z_pieces[5], z_pieces[6]))
    farthest = permute(far, other_core)
    *attended, gradient = layer(
        place, (normed, near, far, farthest), z_pieces, x_pieces, packed, cosine, sine
    )

    returned = [attended[0]] + [permute(v, m) for v, m in zip(attended[1:], OWNERS)]
    terms = lax.all_to_all(gradient.reshape(256, 2, 256), ("owner", "fsdp", "dp"), 0, 0, tiled=True)
    summed = jnp.sum(terms.reshape(4, 64, 2, 2, 128).astype(jnp.float32), axis=1)
    summed = summed.transpose(1, 2, 0, 3).reshape(2, 1024)
    owned = spread(summed.astype(jnp.bfloat16), ("fsdp", "dp"), 64)
    owned = owned.reshape(128, 1024).astype(jnp.float32)
    attention_out = unpack(place, returned)
    new_cartridge, new_first, new_second = adam_update(
        cartridge, adam_first_moment, adam_second_moment, owned
    )
    return attention_out, new_cartridge, new_first, new_second


def solution(mesh):
    placed = (
        P(MESH_AXES, None, None),
        P(),
        P(("fsdp", "dp"), None),
        P(("fsdp", "dp"), None),
        P(MESH_AXES),
        P(MESH_AXES, None, None),
        P("owner", None),
        P("owner", None),
        P("owner", None),
    )
    return jax.shard_map(
        layer_step,
        mesh=mesh,
        in_specs=placed,
        out_specs=(
            P(MESH_AXES, None, None),
            P("owner", None),
            P("owner", None),
            P("owner", None),
        ),
        check_vma=False,
    )
```

profile of v0, /device:TPU:2, one launch (start us, length us, event | category | flops | bytes accessed | tf_op | source)
XLA Modules:
  0.0 212.7 jit_solution(10813934286241735332)
XLA Ops:
  2.4 3.1 %collective-permute-start.2 = (bf16[64,768]{1,0:T(8,128)(2,1)S(1)}, bf16[64,768]{1,0:T(8,128)(2,1)S(1)}, u32[]{:S(2)}, u32[]{:S(2)}) collective-permute-start(bf16[64,768]{1,0:T(8,128)(2,1)S(1)} %get-tuple-element.28), channel_id=1, source_target_pairs={{0,130},{1,131},{2,128},{3,129},{4,134},{5,135},{6,132},{7,133},{8... | collective-permute-start | bytes 294920 | tf_op jit(solution)/shard_map/ppermute | solution.py:32
  5.5 4.3 %shard_map.120.refs_0_ = bf16[256,4096]{1,0:T(8,128)(2,1)} custom-call(bf16[1,256,4096]{2,1,0:T(8,128)(2,1)} %states, f32[1,4096]{1,0:T(1,128)} %bitcast.14), custom_call_target="tpu_custom_call" | custom-call | tf_op jit(solution)/shard_map/pallas_call | solution.py:93
  11.8 4.1 %shard_map.121 = (bf16[320,512]{1,0:T(8,128)(2,1)}, bf16[320,512]{1,0:T(8,128)(2,1)}, bf16[320,512]{1,0:T(8,128)(2,1)}, bf16[320,512]{1,0:T(8,128)(2,1)}) custom-call(s32[5]{0:T(128)} %stack.34.place, bf16[1,256,2048]{2,1,0:T(8,128)(2,1)} %cotangent.1, f32[128,1024]{1,0:T(8,128)} %value_rows.1, f32[128,1024]{1,0:T(8,128)} %value_rows.1), custom_call_target="tpu_custom_call" | custom-call | tf_op jit(solution)/shard_map/pallas_call | solution.py:127
  16.8 2.2 %collective-permute-start.4 = (bf16[128,384]{1,0:T(8,128)(2,1)S(1)}, bf16[128,384]{1,0:T(8,128)(2,1)S(1)}, u32[]{:S(2)}, u32[]{:S(2)}) collective-permute-start(bf16[128,384]{1,0:T(8,128)(2,1)S(1)} %get-tuple-element.55), channel_id=1, source_target_pairs={{0,64},{1,65},{2,66},{3,67},{4,68},{5,69},{6,70},{7,71},{8,72},{9,... | collective-permute-start | bytes 294920 | tf_op jit(solution)/shard_map/ppermute | solution.py:32
  19.0 2.0 collective-permute-start.5
  21.0 2.8 %collective-permute-done.4 = bf16[128,384]{1,0:T(8,128)(2,1)S(1)} collective-permute-done((bf16[128,384]{1,0:T(8,128)(2,1)S(1)}, bf16[128,384]{1,0:T(8,128)(2,1)S(1)}, u32[]{:S(2)}, u32[]{:S(2)}) %collective-permute-start.4) | collective-permute-done | bytes 98336 | tf_op jit(solution)/shard_map/ppermute | solution.py:32
  24.8 5.9 %collective-permute-start.9 = (bf16[4,128,384]{2,1,0:T(8,128)(2,1)S(1)}, bf16[4,128,384]{2,1,0:T(8,128)(2,1)}, u32[]{:S(2)}, u32[]{:S(2)}) collective-permute-start(bf16[4,128,384]{2,1,0:T(8,128)(2,1)S(1)} %pad_maximum_fusion.refs_4_), channel_id=1, source_target_pairs={{0,28},{1,29},{2,30},{3,31},{4,0},{5,1},{6,2},{7,3},{8,4},{9,5},{1... | collective-permute-start | bytes 1179656 | tf_op jit(solution)/shard_map/ppermute | solution.py:32
  30.7 0.9 broadcast_in_dim.4
  31.7 4.6 %all-to-all-start = ((bf16[8,128,384]{2,1,0:T(8,128)(2,1)}), bf16[8,128,384]{2,1,0:T(8,128)(2,1)S(1)}, u32[]{:S(2)}, u32[]{:S(2)}) async-start(bf16[8,128,384]{2,1,0:T(8,128)(2,1)} %broadcast_in_dim.4), calls=%async_computation | async-start | bytes 1572864 | tf_op jit(solution)/shard_map/all_to_all | solution.py:65
  36.3 5.4 %collective-permute-done.9.refs_6_ = bf16[4,128,384]{2,1,0:T(8,128)(2,1)} collective-permute-done((bf16[4,128,384]{2,1,0:T(8,128)(2,1)S(1)}, bf16[4,128,384]{2,1,0:T(8,128)(2,1)}, u32[]{:S(2)}, u32[]{:S(2)}) %collective-permute-start.9) | collective-permute-done | bytes 393248 | tf_op jit(solution)/shard_map/ppermute | solution.py:32
  41.7 4.4 %collective-permute-start.10 = (bf16[4,128,384]{2,1,0:T(8,128)(2,1)}, bf16[4,128,384]{2,1,0:T(8,128)(2,1)S(1)}, u32[]{:S(2)}, u32[]{:S(2)}) collective-permute-start(bf16[4,128,384]{2,1,0:T(8,128)(2,1)} %collective-permute-done.9.refs_6_), channel_id=1, source_target_pairs={{0,28},{1,29},{2,30},{3,31},{4,0},{5,1},{6,2},{7,3},{8,4},{9,5},{1... | collective-permute-start | bytes 1179656 | tf_op jit(solution)/shard_map/ppermute | solution.py:32
  46.1 2.0 collective-permute-done.6.refs_5_
  48.1 16.0 %collective-permute-done.10.refs_8_ = bf16[4,128,384]{2,1,0:T(8,128)(2,1)S(1)} collective-permute-done((bf16[4,128,384]{2,1,0:T(8,128)(2,1)}, bf16[4,128,384]{2,1,0:T(8,128)(2,1)S(1)}, u32[]{:S(2)}, u32[]{:S(2)}) %collective-permute-start.10) | collective-permute-done | bytes 393248 | tf_op jit(solution)/shard_map/ppermute | solution.py:32
  64.1 3.6 %collective-permute-start.11 = (bf16[4,128,384]{2,1,0:T(8,128)(2,1)S(1)}, bf16[4,128,384]{2,1,0:T(8,128)(2,1)S(1)}, u32[]{:S(2)}, u32[]{:S(2)}) collective-permute-start(bf16[4,128,384]{2,1,0:T(8,128)(2,1)S(1)} %collective-permute-done.10.refs_8_), channel_id=1, source_target_pairs={{0,28},{1,29},{2,30},{3,31},{4,0},{5,1},{6,2},{7,3},{8,4},{9,5},{1... | collective-permute-start | bytes 1179656 | tf_op jit(solution)/shard_map/ppermute | solution.py:32
  67.8 7.0 %collective-permute-done.11.refs_10_ = bf16[4,128,384]{2,1,0:T(8,128)(2,1)S(1)} collective-permute-done((bf16[4,128,384]{2,1,0:T(8,128)(2,1)S(1)}, bf16[4,128,384]{2,1,0:T(8,128)(2,1)S(1)}, u32[]{:S(2)}, u32[]{:S(2)}) %collective-permute-start.11) | collective-permute-done | bytes 393248 | tf_op jit(solution)/shard_map/ppermute | solution.py:32
  74.8 3.4 %collective-permute-done.8.refs_9_ = bf16[4,128,384]{2,1,0:T(8,128)(2,1)S(1)} collective-permute-done((bf16[4,128,384]{2,1,0:T(8,128)(2,1)S(1)}, bf16[4,128,384]{2,1,0:T(8,128)(2,1)S(1)}, u32[]{:S(2)}, u32[]{:S(2)}) %collective-permute-start.8) | collective-permute-done | bytes 393248 | tf_op jit(solution)/shard_map/ppermute | solution.py:32
  79.1 2.0 collective-permute-start.14
  81.1 17.8 %collective-permute-done.15.refs_14_ = bf16[8,128,384]{2,1,0:T(8,128)(2,1)S(1)} collective-permute-done((bf16[8,128,384]{2,1,0:T(8,128)(2,1)S(1)}, bf16[8,128,384]{2,1,0:T(8,128)(2,1)S(1)}, u32[]{:S(2)}, u32[]{:S(2)}) %collective-permute-start.15) | collective-permute-done | bytes 786464 | tf_op jit(solution)/shard_map/ppermute | solution.py:32
  100.4 9.4 %collective-permute-done.19.refs_19_ = bf16[320,512]{1,0:T(8,128)(2,1)S(1)} collective-permute-done((bf16[320,512]{1,0:T(8,128)(2,1)}, bf16[320,512]{1,0:T(8,128)(2,1)S(1)}, u32[]{:S(2)}, u32[]{:S(2)}) %collective-permute-start.19) | collective-permute-done | bytes 327712 | tf_op jit(solution)/shard_map/ppermute | solution.py:32
  110.0 3.9 %collective-permute-done.20.refs_20_ = bf16[320,512]{1,0:T(8,128)(2,1)S(1)} collective-permute-done((bf16[320,512]{1,0:T(8,128)(2,1)}, bf16[320,512]{1,0:T(8,128)(2,1)S(1)}, u32[]{:S(2)}, u32[]{:S(2)}) %collective-permute-start.20) | collective-permute-done | bytes 327712 | tf_op jit(solution)/shard_map/ppermute | solution.py:32
  114.0 1.3 collective-permute-start.16
  115.3 2.8 %collective-permute-done.17.refs_16_ = bf16[4,128,384]{2,1,0:T(8,128)(2,1)S(1)} collective-permute-done((bf16[4,128,384]{2,1,0:T(8,128)(2,1)S(1)}, bf16[4,128,384]{2,1,0:T(8,128)(2,1)S(1)}, u32[]{:S(2)}, u32[]{:S(2)}) %collective-permute-start.17) | collective-permute-done | bytes 393248 | tf_op jit(solution)/shard_map/ppermute | solution.py:32
  118.1 7.3 %collective-permute-done.16.refs_15_ = bf16[4,128,384]{2,1,0:T(8,128)(2,1)S(1)} collective-permute-done((bf16[4,128,384]{2,1,0:T(8,128)(2,1)S(1)}, bf16[4,128,384]{2,1,0:T(8,128)(2,1)S(1)}, u32[]{:S(2)}, u32[]{:S(2)}) %collective-permute-start.16) | collective-permute-done | bytes 393248 | tf_op jit(solution)/shard_map/ppermute | solution.py:32
  126.2 32.1 %shard_map.122 = (bf16[256,512]{1,0:T(8,128)(2,1)}, bf16[256,512]{1,0:T(8,128)(2,1)}, bf16[256,512]{1,0:T(8,128)(2,1)}, bf16[256,512]{1,0:T(8,128)(2,1)}, bf16[512,256]{1,0:T(8,128)(2,1)}) custom-call(s32[5]{0:T(128)} %stack.34.place, bf16[256,4096]{1,0:T(8,128)(2,1)} %shard_map.120.refs_0_, bf16[256,4096]{1,0:T(8,128)(2,1)} %collective-permute-done.refs_1_, ...), custom_call_target="tpu_custom_call" | custom-call | tf_op jit(solution)/shard_map/pallas_call | solution.py:317
  158.4 1.1 reshape.40
  159.5 23.9 %all_to_all.15 = bf16[256,2,256]{2,1,0:T(2,128)(2,1)S(1)} all-to-all(bf16[256,2,256]{2,1,0:T(2,128)(2,1)S(1)} %reshape.40), channel_id=1, replica_groups=mesh['fsdp'=2,'dp'=32,'owner'=4] {'owner','fsdp','dp'}, dimensions={0} | all-to-all | bytes 524288 | tf_op jit(solution)/shard_map/all_to_all | solution.py:420
  184.7 6.1 %all-to-all-start.2 = ((bf16[64,2,1024]{2,1,0:T(2,128)(2,1)}), bf16[64,2,1024]{2,1,0:T(2,128)(2,1)S(1)}, u32[]{:S(2)}, u32[]{:S(2)}) async-start(bf16[64,2,1024]{2,1,0:T(2,128)(2,1)} %broadcast_in_dim.5), calls=%async_computation.2 | async-start | bytes 524288 | tf_op jit(solution)/shard_map/all_to_all | solution.py:65
  191.5 1.3 collective-permute-start.23
  192.8 9.5 %collective-permute-done.22.refs_2_ = bf16[256,512]{1,0:T(8,128)(2,1)S(1)} collective-permute-done((bf16[256,512]{1,0:T(8,128)(2,1)S(1)}, bf16[256,512]{1,0:T(8,128)(2,1)S(1)}, u32[]{:S(2)}, u32[]{:S(2)}) %collective-permute-start.22) | collective-permute-done | bytes 262176 | tf_op jit(solution)/shard_map/ppermute | solution.py:32
  202.4 4.8 %collective-permute-done.23.refs_3_ = bf16[256,512]{1,0:T(8,128)(2,1)S(1)} collective-permute-done((bf16[256,512]{1,0:T(8,128)(2,1)S(1)}, bf16[256,512]{1,0:T(8,128)(2,1)S(1)}, u32[]{:S(2)}, u32[]{:S(2)}) %collective-permute-start.23) | collective-permute-done | bytes 262176 | tf_op jit(solution)/shard_map/ppermute | solution.py:32
  207.8 3.4 %shard_map.123 = bf16[1,256,2048]{2,1,0:T(8,128)(2,1)} custom-call(s32[5]{0:T(128)} %stack.34.place, bf16[256,512]{1,0:T(8,128)(2,1)} %get-tuple-element.43.refs_0_, bf16[256,512]{1,0:T(8,128)(2,1)} %copy-done.18, bf16[256,512]{1,0:T(8,128)(2,1)} %copy-done.19, bf16[256,512]{1,0:T(8,128)(2,1)} %copy-done.20), custom_call_target="tpu_custom_call" | custom-call | tf_op jit(solution)/shard_map/pallas_call | solution.py:153
  211.4 1.4 divide_subtract_fusion
  (96 shorter events, 11.0 us)
Async XLA Ops:
  2.4 14.4 %collective-permute-start.2 = (bf16[64,768]{1,0:T(8,128)(2,1)S(1)}, bf16[64,768]{1,0:T(8,128)(2,1)S(1)}, u32[]{:S(2)}, u32[]{:S(2)}) collective-permute-start(bf16[64,768]{1,0:T(8,128)(2,1)S(1)} %get-tuple-element.28), channel_id=1, source_target_pairs={{0,130},{1,131},{2,128},{3,129},{4,134},{5,135},{6,132},{7,133},{8... | collective-permute-start | bytes 294920 | tf_op jit(solution)/shard_map/ppermute | solution.py:32
  9.7 68.5 %collective-permute-start.1 = (bf16[256,4096]{1,0:T(8,128)(2,1)}, bf16[256,4096]{1,0:T(8,128)(2,1)}, u32[]{:S(2)}, u32[]{:S(2)}) collective-permute-start(bf16[256,4096]{1,0:T(8,128)(2,1)} %shard_map.120.refs_0_), channel_id=1, source_target_pairs={{0,2},{1,3},{2,0},{3,1},{4,6},{5,7},{6,4},{7,5},{8,10},{9,11},{10,... | collective-permute-start | bytes 6291464 | tf_op jit(solution)/shard_map/ppermute | solution.py:32
  16.7 51.0 %copy-start = (bf16[256,4096]{1,0:T(8,128)(2,1)S(1)}, bf16[256,4096]{1,0:T(8,128)(2,1)}, u32[]{:S(2)}) copy-start(bf16[256,4096]{1,0:T(8,128)(2,1)} %shard_map.120.refs_0_) | copy-start | bytes 6291460
  16.8 7.0 %collective-permute-start.4 = (bf16[128,384]{1,0:T(8,128)(2,1)S(1)}, bf16[128,384]{1,0:T(8,128)(2,1)S(1)}, u32[]{:S(2)}, u32[]{:S(2)}) collective-permute-start(bf16[128,384]{1,0:T(8,128)(2,1)S(1)} %get-tuple-element.55), channel_id=1, source_target_pairs={{0,64},{1,65},{2,66},{3,67},{4,68},{5,69},{6,70},{7,71},{8,72},{9,... | collective-permute-start | bytes 294920 | tf_op jit(solution)/shard_map/ppermute | solution.py:32
  19.0 5.7 %collective-permute-start.3 = (bf16[128,384]{1,0:T(8,128)(2,1)S(1)}, bf16[128,384]{1,0:T(8,128)(2,1)S(1)}, u32[]{:S(2)}, u32[]{:S(2)}) collective-permute-start(bf16[128,384]{1,0:T(8,128)(2,1)S(1)} %get-tuple-element.55), channel_id=1, source_target_pairs={{0,32},{1,33},{2,34},{3,35},{4,36},{5,37},{6,38},{7,39},{8,40},{9,... | collective-permute-start | bytes 294920 | tf_op jit(solution)/shard_map/ppermute | solution.py:32
  19.0 5.7 %collective-permute-start.5 = (bf16[128,384]{1,0:T(8,128)(2,1)S(1)}, bf16[128,384]{1,0:T(8,128)(2,1)S(1)}, u32[]{:S(2)}, u32[]{:S(2)}) collective-permute-start(bf16[128,384]{1,0:T(8,128)(2,1)S(1)} %get-tuple-element.55), channel_id=1, source_target_pairs={{0,96},{1,97},{2,98},{3,99},{4,100},{5,101},{6,102},{7,103},{8,104... | collective-permute-start | bytes 294920 | tf_op jit(solution)/shard_map/ppermute | solution.py:32
  24.8 101.5 %copy-start.5 = (bf16[4,128,384]{2,1,0:T(8,128)(2,1)}, bf16[4,128,384]{2,1,0:T(8,128)(2,1)S(1)}, u32[]{:S(2)}) copy-start(bf16[4,128,384]{2,1,0:T(8,128)(2,1)S(1)} %pad_maximum_fusion.refs_4_) | copy-start | bytes 1179652
  24.8 16.9 %collective-permute-start.9 = (bf16[4,128,384]{2,1,0:T(8,128)(2,1)S(1)}, bf16[4,128,384]{2,1,0:T(8,128)(2,1)}, u32[]{:S(2)}, u32[]{:S(2)}) collective-permute-start(bf16[4,128,384]{2,1,0:T(8,128)(2,1)S(1)} %pad_maximum_fusion.refs_4_), channel_id=1, source_target_pairs={{0,28},{1,29},{2,30},{3,31},{4,0},{5,1},{6,2},{7,3},{8,4},{9,5},{1... | collective-permute-start | bytes 1179656 | tf_op jit(solution)/shard_map/ppermute | solution.py:32
  30.7 17.4 %collective-permute-start.6 = (bf16[4,128,384]{2,1,0:T(8,128)(2,1)S(1)}, bf16[4,128,384]{2,1,0:T(8,128)(2,1)}, u32[]{:S(2)}, u32[]{:S(2)}) collective-permute-start(bf16[4,128,384]{2,1,0:T(8,128)(2,1)S(1)} %pad_maximum_fusion.refs_4_), channel_id=1, source_target_pairs={{0,4},{1,5},{2,6},{3,7},{4,8},{5,9},{6,10},{7,11},{8,12},{9,13},{1... | collective-permute-start | bytes 1179656 | tf_op jit(solution)/shard_map/ppermute | solution.py:32
  31.7 47.3 %all-to-all-start = ((bf16[8,128,384]{2,1,0:T(8,128)(2,1)}), bf16[8,128,384]{2,1,0:T(8,128)(2,1)S(1)}, u32[]{:S(2)}, u32[]{:S(2)}) async-start(bf16[8,128,384]{2,1,0:T(8,128)(2,1)} %broadcast_in_dim.4), calls=%async_computation | async-start | bytes 1572864 | tf_op jit(solution)/shard_map/all_to_all | solution.py:65
  41.7 22.4 %collective-permute-start.10 = (bf16[4,128,384]{2,1,0:T(8,128)(2,1)}, bf16[4,128,384]{2,1,0:T(8,128)(2,1)S(1)}, u32[]{:S(2)}, u32[]{:S(2)}) collective-permute-start(bf16[4,128,384]{2,1,0:T(8,128)(2,1)} %collective-permute-done.9.refs_6_), channel_id=1, source_target_pairs={{0,28},{1,29},{2,30},{3,31},{4,0},{5,1},{6,2},{7,3},{8,4},{9,5},{1... | collective-permute-start | bytes 1179656 | tf_op jit(solution)/shard_map/ppermute | solution.py:32
  48.1 19.6 %collective-permute-start.7 = (bf16[4,128,384]{2,1,0:T(8,128)(2,1)}, bf16[4,128,384]{2,1,0:T(8,128)(2,1)S(1)}, u32[]{:S(2)}, u32[]{:S(2)}) collective-permute-start(bf16[4,128,384]{2,1,0:T(8,128)(2,1)} %collective-permute-done.6.refs_5_), channel_id=1, source_target_pairs={{0,4},{1,5},{2,6},{3,7},{4,8},{5,9},{6,10},{7,11},{8,12},{9,13},{1... | collective-permute-start | bytes 1179656 | tf_op jit(solution)/shard_map/ppermute | solution.py:32
  64.1 10.7 %collective-permute-start.11 = (bf16[4,128,384]{2,1,0:T(8,128)(2,1)S(1)}, bf16[4,128,384]{2,1,0:T(8,128)(2,1)S(1)}, u32[]{:S(2)}, u32[]{:S(2)}) collective-permute-start(bf16[4,128,384]{2,1,0:T(8,128)(2,1)S(1)} %collective-permute-done.10.refs_8_), channel_id=1, source_target_pairs={{0,28},{1,29},{2,30},{3,31},{4,0},{5,1},{6,2},{7,3},{8,4},{9,5},{1... | collective-permute-start | bytes 1179656 | tf_op jit(solution)/shard_map/ppermute | solution.py:32
  67.7 10.6 %collective-permute-start.8 = (bf16[4,128,384]{2,1,0:T(8,128)(2,1)S(1)}, bf16[4,128,384]{2,1,0:T(8,128)(2,1)S(1)}, u32[]{:S(2)}, u32[]{:S(2)}) collective-permute-start(bf16[4,128,384]{2,1,0:T(8,128)(2,1)S(1)} %collective-permute-done.7.refs_7_), channel_id=1, source_target_pairs={{0,4},{1,5},{2,6},{3,7},{4,8},{5,9},{6,10},{7,11},{8,12},{9,13},{1... | collective-permute-start | bytes 1179656 | tf_op jit(solution)/shard_map/ppermute | solution.py:32
  67.7 47.6 %collective-permute-start = (bf16[256,4096]{1,0:T(8,128)(2,1)S(1)}, bf16[256,4096]{1,0:T(8,128)(2,1)}, u32[]{:S(2)}, u32[]{:S(2)}) collective-permute-start(bf16[256,4096]{1,0:T(8,128)(2,1)S(1)} %copy-done), channel_id=1, source_target_pairs={{0,1},{1,0},{2,3},{3,2},{4,5},{5,4},{6,7},{7,6},{8,9},{9,8},{10,11... | collective-permute-start | bytes 6291464 | tf_op jit(solution)/shard_map/ppermute | solution.py:32
  79.0 47.2 %collective-permute-start.12 = (bf16[256,4096]{1,0:T(8,128)(2,1)}, bf16[256,4096]{1,0:T(8,128)(2,1)}, u32[]{:S(2)}, u32[]{:S(2)}) collective-permute-start(bf16[256,4096]{1,0:T(8,128)(2,1)} %collective-permute-done.1.refs_2_), channel_id=1, source_target_pairs={{0,1},{1,0},{2,3},{3,2},{4,5},{5,4},{6,7},{7,6},{8,9},{9,8},{10,11... | collective-permute-start | bytes 6291464 | tf_op jit(solution)/shard_map/ppermute | solution.py:32
  79.0 47.2 %copy-start.2 = (bf16[8,128,384]{2,1,0:T(8,128)(2,1)}, bf16[8,128,384]{2,1,0:T(8,128)(2,1)S(1)}, u32[]{:S(2)}) copy-start(bf16[8,128,384]{2,1,0:T(8,128)(2,1)S(1)} %all-to-all-done.refs_12_) | copy-start | bytes 2359300
  79.0 20.0 %collective-permute-start.15 = (bf16[8,128,384]{2,1,0:T(8,128)(2,1)S(1)}, bf16[8,128,384]{2,1,0:T(8,128)(2,1)S(1)}, u32[]{:S(2)}, u32[]{:S(2)}) collective-permute-start(bf16[8,128,384]{2,1,0:T(8,128)(2,1)S(1)} %all-to-all-done.refs_12_), channel_id=1, source_target_pairs={{0,96},{1,97},{2,98},{3,99},{4,100},{5,101},{6,102},{7,103},{8,104... | collective-permute-start | bytes 2359304 | tf_op jit(solution)/shard_map/ppermute | solution.py:32
  79.1 20.4 %collective-permute-start.14 = (bf16[8,128,384]{2,1,0:T(8,128)(2,1)S(1)}, bf16[8,128,384]{2,1,0:T(8,128)(2,1)S(1)}, u32[]{:S(2)}, u32[]{:S(2)}) collective-permute-start(bf16[8,128,384]{2,1,0:T(8,128)(2,1)S(1)} %all-to-all-done.refs_12_), channel_id=1, source_target_pairs={{0,32},{1,33},{2,34},{3,35},{4,36},{5,37},{6,38},{7,39},{8,40},{9,... | collective-permute-start | bytes 2359304 | tf_op jit(solution)/shard_map/ppermute | solution.py:32
  81.1 19.2 %collective-permute-start.18 = (bf16[320,512]{1,0:T(8,128)(2,1)}, bf16[320,512]{1,0:T(8,128)(2,1)S(1)}, u32[]{:S(2)}, u32[]{:S(2)}) collective-permute-start(bf16[320,512]{1,0:T(8,128)(2,1)} %get-tuple-element.38), channel_id=1, source_target_pairs={{0,1},{1,0},{2,3},{3,2},{4,5},{5,4},{6,7},{7,6},{8,9},{9,8},{10,11... | collective-permute-start | bytes 983048 | tf_op jit(solution)/shard_map/ppermute | solution.py:32
  99.0 10.8 %collective-permute-start.19 = (bf16[320,512]{1,0:T(8,128)(2,1)}, bf16[320,512]{1,0:T(8,128)(2,1)S(1)}, u32[]{:S(2)}, u32[]{:S(2)}) collective-permute-start(bf16[320,512]{1,0:T(8,128)(2,1)} %get-tuple-element.39), channel_id=1, source_target_pairs={{0,2},{1,3},{2,0},{3,1},{4,6},{5,7},{6,4},{7,5},{8,10},{9,11},{10,... | collective-permute-start | bytes 983048 | tf_op jit(solution)/shard_map/ppermute | solution.py:32
  99.5 14.4 %collective-permute-start.20 = (bf16[320,512]{1,0:T(8,128)(2,1)}, bf16[320,512]{1,0:T(8,128)(2,1)S(1)}, u32[]{:S(2)}, u32[]{:S(2)}) collective-permute-start(bf16[320,512]{1,0:T(8,128)(2,1)} %get-tuple-element.40), channel_id=1, source_target_pairs={{0,3},{1,2},{2,1},{3,0},{4,7},{5,6},{6,5},{7,4},{8,11},{9,10},{10,... | collective-permute-start | bytes 983048 | tf_op jit(solution)/shard_map/ppermute | solution.py:32
  100.3 15.0 %collective-permute-start.13 = (bf16[4,128,384]{2,1,0:T(8,128)(2,1)}, bf16[4,128,384]{2,1,0:T(8,128)(2,1)S(1)}, u32[]{:S(2)}, u32[]{:S(2)}) collective-permute-start(bf16[4,128,384]{2,1,0:T(8,128)(2,1)} %copy-done.11), channel_id=1, source_target_pairs={{0,4},{1,5},{2,6},{3,7},{4,8},{5,9},{6,10},{7,11},{8,12},{9,13},{1... | collective-permute-start | bytes 1179656 | tf_op jit(solution)/shard_map/ppermute | solution.py:32
  109.8 8.3 %collective-permute-start.17 = (bf16[4,128,384]{2,1,0:T(8,128)(2,1)S(1)}, bf16[4,128,384]{2,1,0:T(8,128)(2,1)S(1)}, u32[]{:S(2)}, u32[]{:S(2)}) collective-permute-start(bf16[4,128,384]{2,1,0:T(8,128)(2,1)S(1)} %slice.19), channel_id=1, source_target_pairs={{0,96},{1,97},{2,98},{3,99},{4,100},{5,101},{6,102},{7,103},{8,104... | collective-permute-start | bytes 1179656 | tf_op jit(solution)/shard_map/ppermute | solution.py:32
  114.0 11.4 %collective-permute-start.16 = (bf16[4,128,384]{2,1,0:T(8,128)(2,1)S(1)}, bf16[4,128,384]{2,1,0:T(8,128)(2,1)S(1)}, u32[]{:S(2)}, u32[]{:S(2)}) collective-permute-start(bf16[4,128,384]{2,1,0:T(8,128)(2,1)S(1)} %slice.18), channel_id=1, source_target_pairs={{0,32},{1,33},{2,34},{3,35},{4,36},{5,37},{6,38},{7,39},{8,40},{9,... | collective-permute-start | bytes 1179656 | tf_op jit(solution)/shard_map/ppermute | solution.py:32
  158.4 32.5 %copy-start.23 = (bf16[256,512]{1,0:T(8,128)(2,1)S(1)}, bf16[256,512]{1,0:T(8,128)(2,1)}, u32[]{:S(2)}) copy-start(bf16[256,512]{1,0:T(8,128)(2,1)} %get-tuple-element.44) | copy-start | bytes 786436
  158.4 32.6 %copy-start.22 = (bf16[256,512]{1,0:T(8,128)(2,1)S(1)}, bf16[256,512]{1,0:T(8,128)(2,1)}, u32[]{:S(2)}) copy-start(bf16[256,512]{1,0:T(8,128)(2,1)} %get-tuple-element.45) | copy-start | bytes 786436
  158.4 33.1 %copy-start.21 = (bf16[256,512]{1,0:T(8,128)(2,1)S(1)}, bf16[256,512]{1,0:T(8,128)(2,1)}, u32[]{:S(2)}) copy-start(bf16[256,512]{1,0:T(8,128)(2,1)} %get-tuple-element.46) | copy-start | bytes 786436
  184.7 26.6 %all-to-all-start.2 = ((bf16[64,2,1024]{2,1,0:T(2,128)(2,1)}), bf16[64,2,1024]{2,1,0:T(2,128)(2,1)S(1)}, u32[]{:S(2)}, u32[]{:S(2)}) async-start(bf16[64,2,1024]{2,1,0:T(2,128)(2,1)} %broadcast_in_dim.5), calls=%async_computation.2 | async-start | bytes 524288 | tf_op jit(solution)/shard_map/all_to_all | solution.py:65
  190.9 2.0 collective-permute-start.21
  191.0 11.4 %collective-permute-start.22 = (bf16[256,512]{1,0:T(8,128)(2,1)S(1)}, bf16[256,512]{1,0:T(8,128)(2,1)S(1)}, u32[]{:S(2)}, u32[]{:S(2)}) collective-permute-start(bf16[256,512]{1,0:T(8,128)(2,1)S(1)} %copy-done.22), channel_id=1, source_target_pairs={{0,2},{1,3},{2,0},{3,1},{4,6},{5,7},{6,4},{7,5},{8,10},{9,11},{10,... | collective-permute-start | bytes 786440 | tf_op jit(solution)/shard_map/ppermute | solution.py:32
  191.5 15.6 %collective-permute-start.23 = (bf16[256,512]{1,0:T(8,128)(2,1)S(1)}, bf16[256,512]{1,0:T(8,128)(2,1)S(1)}, u32[]{:S(2)}, u32[]{:S(2)}) collective-permute-start(bf16[256,512]{1,0:T(8,128)(2,1)S(1)} %copy-done.21), channel_id=1, source_target_pairs={{0,3},{1,2},{2,1},{3,0},{4,7},{5,6},{6,5},{7,4},{8,11},{9,10},{10,... | collective-permute-start | bytes 786440 | tf_op jit(solution)/shard_map/ppermute | solution.py:32
  (18 other events, 237.5 us)
where the time goes:
time: 215 us; the launch traced here: 213 us
  waiting for transfers between devices  93.1 us (43%)
  Pallas kernels  43.9 us (20%)
  starting transfers between devices  39.2 us (18%)
  blocking collectives  23.9 us (11%)
  local copies, waits for them, and re-layouts  7.91 us (4%)
  other arithmetic  3.04 us (1%)
    ppermute x24, waiting for transfers between devices, permute(): return lax.ppermute(value, MESH_AXES, pairs)  93.1 us
    pallas_call x1, Pallas kernels, layer(): pl.pallas_call(layer_kernel, grid_spec=pltpu.PrefetchScalarGridSpec(num_s...  32.1 us
    ppermute x24, starting transfers between devices, permute(): return lax.ppermute(value, MESH_AXES, pairs)  28.4 us
    all_to_all x1, blocking collectives, layer_step(): lax.all_to_all(gradient.reshape(256, 2, 256), ('owner', 'fsdp', 'dp'), 0,...  23.9 us
    all_to_all x2, starting transfers between devices, spread(): lax.all_to_all(copies, axes, 0, 0, axis_index_groups=groups, tiled=True)  10.8 us
  transfers between devices with their start and end apart: 26, of which 14 were waited for; matrix products, arithmetic and copies ran while one was open for 2% of the time, Pallas kernels for 6%

commit v1 on v0

--- a/solution.py
+++ b/solution.py
@@ -57,12 +57,11 @@
 
 
 OWNERS = (other_core, pair_chip, other_pair)
-Z_GROUPS = [[x * Z_SIZE + z for z in range(Z_SIZE)] for x in range(X_SIZE)]
-
-
-def spread(value, axes, members, groups=None):
+
+
+def spread(value, axes, members):
     copies = jnp.broadcast_to(value[None], (members,) + value.shape)
-    return lax.all_to_all(copies, axes, 0, 0, axis_index_groups=groups, tiled=True)
+    return lax.all_to_all(copies, axes, 0, 0, tiled=True)
 
 
 def rope_tables():
@@ -92,12 +91,12 @@
 def normalise(hidden, gain):
     return pl.pallas_call(
         norm_kernel,
-        grid=(4,),
+        grid=(8,),
         in_specs=[
-            pl.BlockSpec((1, 64, WIDTH), lambda i: (0, i, 0)),
+            pl.BlockSpec((1, 32, WIDTH), lambda i: (0, i, 0)),
             pl.BlockSpec((1, WIDTH), lambda i: (0, 0)),
         ],
-        out_specs=pl.BlockSpec((64, WIDTH), lambda i: (i, 0)),
+        out_specs=pl.BlockSpec((32, WIDTH), lambda i: (i, 0)),
         out_shape=jax.ShapeDtypeStruct((ROWS, WIDTH), jnp.bfloat16),
     )(hidden, gain.reshape(1, WIDTH))
 
@@ -165,10 +164,10 @@
 def layer_kernel(place, *refs):
     states = refs[0:4]
     z_pieces = refs[4:12]
-    x_pieces = refs[12:17]
-    packed, cosine, sine = refs[17:21], refs[21], refs[22]
-    outs, gradient = refs[23:27], refs[27]
-    weights, rows, keys, values, ups, out, sums, piece_sem, row_sem, up_sem = refs[28:]
+    x_pieces = refs[12:20]
+    packed, cosine, sine = refs[20:24], refs[24], refs[25]
+    outs, gradient = refs[26:30], refs[30]
+    weights, rows, keys, values, ups, out, sums, piece_sem, row_sem, up_sem = refs[31:]
     step = pl.program_id(0)
     y_hi, x, z = place[1], place[2], place[3]
 
@@ -181,32 +180,20 @@
             )
 
         offsets = (0, -1, 1, -2, 2, -3, 3, 4)
-        for side in range(2):
-            y_from = y_hi if side == 0 else 1 - y_hi
-            part = pl.ds(side * 64, 64)
-            for piece, offset in zip(z_pieces, offsets):
-                z_from = lax.rem(z + (offset + Z_SIZE), Z_SIZE)
-                for back in range(X_SIZE):
-                    x_from = lax.rem(x + (X_SIZE - back), X_SIZE)
-                    add(
-                        piece.at[back, part, :],
-                        weights.at[y_from, x_from, z_from, :, pl.ds(0, HALF)],
-                    )
-            for piece, offset in zip(x_pieces[:3], (0, -1, 1)):
-                x_from = lax.rem(x + (offset + X_SIZE), X_SIZE)
+        for piece, offset in zip(z_pieces, offsets):
+            z_from = lax.rem(z + (offset + Z_SIZE), Z_SIZE)
+            for back in range(X_SIZE):
+                x_from = lax.rem(x + (X_SIZE - back), X_SIZE)
+                add(piece.at[back], weights.at[:, x_from, z_from, :, pl.ds(0, HALF)])
+        for index, offset in enumerate((0, -1, 1, 2)):
+            x_from = lax.rem(x + (offset + X_SIZE), X_SIZE)
+            for order in range(Z_SIZE):
+                z_from = lax.rem(z + (offsets[order] + Z_SIZE), Z_SIZE)
+                piece = x_pieces[2 * index + (order >= 3)]
                 add(
-                    piece.at[:, part, :],
-                    weights.at[y_from, x_from, :, :, pl.ds(HALF, HALF)],
+                    piece.at[order - 3 if order >= 3 else order],
+                    weights.at[:, x_from, z_from, :, pl.ds(HALF, HALF)],
                 )
-            x_from = lax.rem(x + 2, X_SIZE)
-            add(
-                x_pieces[3].at[:, part, :],
-                weights.at[y_from, x_from, pl.ds(0, 4), :, pl.ds(HALF, HALF)],
-            )
-            add(
-                x_pieces[4].at[:, part, :],
-                weights.at[y_from, x_from, pl.ds(4, 4), :, pl.ds(HALF, HALF)],
-            )
         return copies
 
     def row_copy(index):
@@ -248,7 +235,15 @@
             row_copy(index).wait()
 
     slot = lax.rem(step, 2)
-    projected = dot(rows[slot], weights[...].reshape(WIDTH, COLS), 1, 0)
+    projected = sum(
+        dot(
+            rows[slot, :, pl.ds(pl.multiple_of((y_hi ^ side) * 2048, 2048), 2048)],
+            weights[side].reshape(2048, COLS),
+            1,
+            0,
+        )
+        for side in range(2)
+    )
     cos, sin = cosine[...], sine[...]
 
     def rope(v):
@@ -319,7 +314,7 @@
         grid_spec=pltpu.PrefetchScalarGridSpec(
             num_scalar_prefetch=1,
             grid=(4,),
-            in_specs=[anywhere] * 21 + [whole(cosine.shape), whole(sine.shape)],
+            in_specs=[anywhere] * 24 + [whole(cosine.shape), whole(sine.shape)],
             out_specs=[pl.BlockSpec((ROWS, 512), lambda i, place: (0, 0))] * 4
             + [
                 pl.BlockSpec((PREFIX, 256), lambda i, place: (0, 0)),
@@ -332,7 +327,7 @@
                 pltpu.VMEM((4, 320, 512), jnp.bfloat16),
                 pltpu.VMEM((ROWS, 512), jnp.bfloat16),
                 pltpu.VMEM((256, PREFIX), jnp.float32),
-                pltpu.SemaphoreType.DMA((74,)),
+                pltpu.SemaphoreType.DMA((64,)),
                 pltpu.SemaphoreType.DMA((2,)),
                 pltpu.SemaphoreType.DMA((4,)),
             ],
@@ -357,19 +352,27 @@
 
 
 def gather_weights(own, across):
-    both = jnp.concatenate([own, across], axis=0)
-    first = both[:, :HALF]
-    first = jnp.stack([first] + [permute(first, along_x(step)) for step in (1, 2, 3)])
-    second = spread(both[:, HALF:], "dp", Z_SIZE, Z_GROUPS)
-    z_pieces = [first]
-    up, down = first, first
+    both = jnp.stack([own, across])
+    first, second = both[:, :, :HALF], both[:, :, HALF:]
+    ups, downs = [second], [second]
+    for _ in range(3):
+        ups.append(permute(ups[-1], along_z(1)))
+        downs.append(permute(downs[-1], along_z(-1)))
+    last = permute(ups[3], along_z(1))
+    near = jnp.stack([second, ups[1], downs[1]])
+    rest = jnp.stack([ups[2], downs[2], ups[3], downs[3], last])
+    near_up, near_down = permute(near, along_x(1)), permute(near, along_x(-1))
+    rest_up, rest_down = permute(rest, along_x(1)), permute(rest, along_x(-1))
+    near_two = permute(near_up, along_x(1))
+    rest_two = permute(rest_down, along_x(-1))
+    x_pieces = [near, rest, near_up, rest_up, near_down, rest_down, near_two, rest_two]
+    block = jnp.stack([first] + [permute(first, along_x(step)) for step in (1, 2, 3)])
+    z_pieces = [block]
+    up, down = block, block
     for _ in range(3):
         up, down = permute(up, along_z(1)), permute(down, along_z(-1))
         z_pieces += [up, down]
     z_pieces += [permute(up, along_z(1))]
-    up, down = permute(second, along_x(1)), permute(second, along_x(-1))
-    x_pieces = [second, up, down]
-    x_pieces += [permute(up[:4], along_x(1)), permute(down[4:], along_x(-1))]
     return z_pieces, x_pieces
 
 
@@ -406,10 +409,9 @@
     normed = normalise(hidden, norm_gain)
     far = permute(normed, pair_chip)
     near = permute(normed, other_core)
+    z_pieces, x_pieces = gather_weights(own, across)
     packed = pack(place, cotangent, cartridge)
-    across, packed, cosine, sine = lax.optimization_barrier((across, packed, cosine, sine))
-    z_pieces, x_pieces = gather_weights(own, across)
-    packed = [packed[0]] + [permute(v, m) for v, m in zip(packed[1:], OWNERS)]
+    packed = [packed[0]] + [permute(packed[i], OWNERS[i - 1]) for i in (1, 2, 3)]
     far, z_pieces[5], z_pieces[6] = lax.optimization_barrier((far, z_pieces[5], z_pieces[6]))
     farthest = permute(far, other_core)
     *attended, gradient = layer(

time: 215 us -> 217 us (level)
  waiting for transfers between devices: 93.1 us -> 82.4 us
  starting transfers between devices: 39.2 us -> 47.8 us
    ppermute x24 -> x33, starting transfers between devices: 28.4 us -> 41.9 us  [permute(): return lax.ppermute(value, MESH_AXES, pairs)]
    ppermute x24 -> x33, waiting for transfers between devices: 93.1 us -> 82.4 us  [permute(): return lax.ppermute(value, MESH_AXES, pairs)]
    all_to_all x2 -> x1, starting transfers between devices: 10.8 us -> 5.91 us  [spread(): return lax.all_to_all(copies, axes, 0, 0, tiled=True)]
    unnamed x49 -> x56, local copies, waits for them, and re-layouts: 2.27 us -> 4.52 us
  transfers between devices with their start and end apart: 26 -> 34, of which waited for: 14 -> 21; matrix products, arithmetic and copies ran while one was open for 2% -> 2% of each run, Pallas kernels for 6% -> 3%
where the time goes in v1:
time: 217 us; the launch traced here: 215 us
  waiting for transfers between devices  82.4 us (38%)
  starting transfers between devices  47.8 us (22%)
  Pallas kernels  45.7 us (21%)
  blocking collectives  24.6 us (11%)
  local copies, waits for them, and re-layouts  9.1 us (4%)
  other arithmetic  3.99 us (2%)
    ppermute x33, waiting for transfers between devices, permute(): return lax.ppermute(value, MESH_AXES, pairs)  82.4 us
    ppermute x33, starting transfers between devices, permute(): return lax.ppermute(value, MESH_AXES, pairs)  41.9 us
    pallas_call x1, Pallas kernels, layer(): pl.pallas_call(layer_kernel, grid_spec=pltpu.PrefetchScalarGridSpec(num_s...  32 us
    all_to_all x1, blocking collectives, layer_step(): lax.all_to_all(gradient.reshape(256, 2, 256), ('owner', 'fsdp', 'dp'), 0,...  24.6 us
    pallas_call x1, Pallas kernels, normalise(): pl.pallas_call(norm_kernel, grid=(8,), in_specs=[pl.BlockSpec((1, 32, WID...  6.19 us
    all_to_all x1, starting transfers between devices, spread(): return lax.all_to_all(copies, axes, 0, 0, tiled=True)  5.91 us
    unnamed x56, local copies, waits for them, and re-layouts  4.52 us
  transfers between devices with their start and end apart: 34, of which 21 were waited for; matrix products, arithmetic and copies ran while one was open for 2% of the time, Pallas kernels for 3%

profile of v1, /device:TPU:2, one launch (start us, length us, event | category | flops | bytes accessed | tf_op | source)
XLA Modules:
  0.0 215.2 jit_solution(12443572201992590013)
XLA Ops:
  2.4 6.2 %shard_map.120.refs_0_ = bf16[256,4096]{1,0:T(8,128)(2,1)} custom-call(bf16[1,256,4096]{2,1,0:T(8,128)(2,1)} %states, f32[1,4096]{1,0:T(1,128)} %bitcast.33), custom_call_target="tpu_custom_call" | custom-call | tf_op jit(solution)/shard_map/pallas_call | solution.py:92
  8.6 1.6 collective-permute-start.1
  10.1 2.2 %collective-permute-start.2 = (bf16[64,768]{1,0:T(8,128)(2,1)S(1)}, bf16[64,768]{1,0:T(8,128)(2,1)S(1)}, u32[]{:S(2)}, u32[]{:S(2)}) collective-permute-start(bf16[64,768]{1,0:T(8,128)(2,1)S(1)} %get-tuple-element.21), channel_id=1, source_target_pairs={{0,130},{1,131},{2,128},{3,129},{4,134},{5,135},{6,132},{7,133},{8... | collective-permute-start | bytes 294920 | tf_op jit(solution)/shard_map/ppermute | solution.py:32
  12.3 3.6 %collective-permute-done.2 = bf16[64,768]{1,0:T(8,128)(2,1)S(1)} collective-permute-done((bf16[64,768]{1,0:T(8,128)(2,1)S(1)}, bf16[64,768]{1,0:T(8,128)(2,1)S(1)}, u32[]{:S(2)}, u32[]{:S(2)}) %collective-permute-start.2) | collective-permute-done | bytes 98336 | tf_op jit(solution)/shard_map/ppermute | solution.py:32
  16.7 2.3 %collective-permute-start.4 = (bf16[2,64,384]{2,1,0:T(8,128)(2,1)S(1)}, bf16[2,64,384]{2,1,0:T(8,128)(2,1)S(1)}, u32[]{:S(2)}, u32[]{:S(2)}) collective-permute-start(bf16[2,64,384]{2,1,0:T(8,128)(2,1)S(1)} %get-tuple-element.40), channel_id=1, source_target_pairs={{0,64},{1,65},{2,66},{3,67},{4,68},{5,69},{6,70},{7,71},{8,72},{9,... | collective-permute-start | bytes 294920 | tf_op jit(solution)/shard_map/ppermute | solution.py:32
  19.0 1.8 collective-permute-start.3
  21.1 1.7 collective-permute-done.4
  23.9 5.9 %collective-permute-start.9 = (bf16[4,2,64,384]{3,2,1,0:T(8,128)(2,1)S(1)}, bf16[4,2,64,384]{3,2,1,0:T(8,128)(2,1)S(1)}, u32[]{:S(2)}, u32[]{:S(2)}) collective-permute-start(bf16[4,2,64,384]{3,2,1,0:T(8,128)(2,1)S(1)} %pad_maximum_fusion.refs_4_), channel_id=1, source_target_pairs={{0,28},{1,29},{2,30},{3,31},{4,0},{5,1},{6,2},{7,3},{8,4},{9,5},{1... | collective-permute-start | bytes 1179656 | tf_op jit(solution)/shard_map/ppermute | solution.py:32
  29.8 5.9 %collective-permute-done.9.refs_6_ = bf16[4,2,64,384]{3,2,1,0:T(8,128)(2,1)S(1)} collective-permute-done((bf16[4,2,64,384]{3,2,1,0:T(8,128)(2,1)S(1)}, bf16[4,2,64,384]{3,2,1,0:T(8,128)(2,1)S(1)}, u32[]{:S(2)}, u32[]{:S(2)}) %collective-permute-start.9) | collective-permute-done | bytes 393248 | tf_op jit(solution)/shard_map/ppermute | solution.py:32
  35.7 3.7 %collective-permute-start.10 = (bf16[4,2,64,384]{3,2,1,0:T(8,128)(2,1)S(1)}, bf16[4,2,64,384]{3,2,1,0:T(8,128)(2,1)}, u32[]{:S(2)}, u32[]{:S(2)}) collective-permute-start(bf16[4,2,64,384]{3,2,1,0:T(8,128)(2,1)S(1)} %collective-permute-done.9.refs_6_), channel_id=1, source_target_pairs={{0,28},{1,29},{2,30},{3,31},{4,0},{5,1},{6,2},{7,3},{8,4},{9,5},{1... | collective-permute-start | bytes 1179656 | tf_op jit(solution)/shard_map/ppermute | solution.py:32
  39.4 5.8 %collective-permute-done.10.refs_8_ = bf16[4,2,64,384]{3,2,1,0:T(8,128)(2,1)} collective-permute-done((bf16[4,2,64,384]{3,2,1,0:T(8,128)(2,1)S(1)}, bf16[4,2,64,384]{3,2,1,0:T(8,128)(2,1)}, u32[]{:S(2)}, u32[]{:S(2)}) %collective-permute-start.10) | collective-permute-done | bytes 393248 | tf_op jit(solution)/shard_map/ppermute | solution.py:32
  45.2 3.8 %collective-permute-start.11 = (bf16[4,2,64,384]{3,2,1,0:T(8,128)(2,1)}, bf16[4,2,64,384]{3,2,1,0:T(8,128)(2,1)}, u32[]{:S(2)}, u32[]{:S(2)}) collective-permute-start(bf16[4,2,64,384]{3,2,1,0:T(8,128)(2,1)} %collective-permute-done.10.refs_8_), channel_id=1, source_target_pairs={{0,28},{1,29},{2,30},{3,31},{4,0},{5,1},{6,2},{7,3},{8,4},{9,5},{1... | collective-permute-start | bytes 1179656 | tf_op jit(solution)/shard_map/ppermute | solution.py:32
  49.3 3.3 %collective-permute-start.15 = (bf16[2,64,384]{2,1,0:T(8,128)(2,1)S(1)}, bf16[2,64,384]{2,1,0:T(8,128)(2,1)}, u32[]{:S(2)}, u32[]{:S(2)}) collective-permute-start(bf16[2,64,384]{2,1,0:T(8,128)(2,1)S(1)} %get-tuple-element.39), channel_id=1, source_target_pairs={{0,28},{1,29},{2,30},{3,31},{4,0},{5,1},{6,2},{7,3},{8,4},{9,5},{1... | collective-permute-start | bytes 294920 | tf_op jit(solution)/shard_map/ppermute | solution.py:32
  52.6 8.0 %collective-permute-done.14 = bf16[2,64,384]{2,1,0:T(8,128)(2,1)S(1)} collective-permute-done((bf16[2,64,384]{2,1,0:T(8,128)(2,1)S(1)}, bf16[2,64,384]{2,1,0:T(8,128)(2,1)S(1)}, u32[]{:S(2)}, u32[]{:S(2)}) %collective-permute-start.14) | collective-permute-done | bytes 98336 | tf_op jit(solution)/shard_map/ppermute | solution.py:32
  61.9 4.0 %shard_map.121 = (bf16[320,512]{1,0:T(8,128)(2,1)}, bf16[320,512]{1,0:T(8,128)(2,1)}, bf16[320,512]{1,0:T(8,128)(2,1)}, bf16[320,512]{1,0:T(8,128)(2,1)}) custom-call(s32[5]{0:T(128)} %stack.73.place, bf16[1,256,2048]{2,1,0:T(8,128)(2,1)} %cotangent.1, f32[128,1024]{1,0:T(8,128)} %value_rows.1, f32[128,1024]{1,0:T(8,128)} %value_rows.1), custom_call_target="tpu_custom_call" | custom-call | tf_op jit(solution)/shard_map/pallas_call | solution.py:126
  66.7 3.2 %collective-permute-start.17 = (bf16[2,64,384]{2,1,0:T(8,128)(2,1)}, bf16[2,64,384]{2,1,0:T(8,128)(2,1)S(1)}, u32[]{:S(2)}, u32[]{:S(2)}) collective-permute-start(bf16[2,64,384]{2,1,0:T(8,128)(2,1)} %collective-permute-done.15), channel_id=1, source_target_pairs={{0,28},{1,29},{2,30},{3,31},{4,0},{5,1},{6,2},{7,3},{8,4},{9,5},{1... | collective-permute-start | bytes 294920 | tf_op jit(solution)/shard_map/ppermute | solution.py:32
  70.9 1.7 collective-permute-done.17
  72.7 6.4 %collective-permute-done.18 = bf16[2,64,384]{2,1,0:T(8,128)(2,1)S(1)} collective-permute-done((bf16[2,64,384]{2,1,0:T(8,128)(2,1)}, bf16[2,64,384]{2,1,0:T(8,128)(2,1)S(1)}, u32[]{:S(2)}, u32[]{:S(2)}) %collective-permute-start.18) | collective-permute-done | bytes 98336 | tf_op jit(solution)/shard_map/ppermute | solution.py:32
  79.1 2.0 collective-permute-start.19
  81.1 2.6 %collective-permute-done.19 = bf16[2,64,384]{2,1,0:T(8,128)(2,1)S(1)} collective-permute-done((bf16[2,64,384]{2,1,0:T(8,128)(2,1)S(1)}, bf16[2,64,384]{2,1,0:T(8,128)(2,1)S(1)}, u32[]{:S(2)}, u32[]{:S(2)}) %collective-permute-start.19) | collective-permute-done | bytes 98336 | tf_op jit(solution)/shard_map/ppermute | solution.py:32
  83.7 5.8 %collective-permute-done.20 = bf16[2,64,384]{2,1,0:T(8,128)(2,1)S(1)} collective-permute-done((bf16[2,64,384]{2,1,0:T(8,128)(2,1)S(1)}, bf16[2,64,384]{2,1,0:T(8,128)(2,1)S(1)}, u32[]{:S(2)}, u32[]{:S(2)}) %collective-permute-start.20) | collective-permute-done | bytes 98336 | tf_op jit(solution)/shard_map/ppermute | solution.py:32
  89.6 2.8 %collective-permute-start.24 = (bf16[5,2,64,384]{3,2,1,0:T(8,128)(2,1)S(1)}, bf16[5,2,64,384]{3,2,1,0:T(8,128)(2,1)S(1)}, u32[]{:S(2)}, u32[]{:S(2)}) collective-permute-start(bf16[5,2,64,384]{3,2,1,0:T(8,128)(2,1)S(1)} %bitcast_dynamic-update-slice_fusion.refs_13_), channel_id=1, source_target_pairs={{0,96},{1,97},{2,98},{3,99},{4,100},{5,101},{6,102},{7,103},{8,104... | collective-permute-start | bytes 1474568 | tf_op jit(solution)/shard_map/ppermute | solution.py:32
  93.5 6.1 %collective-permute-done.29.refs_23_ = bf16[320,512]{1,0:T(8,128)(2,1)S(1)} collective-permute-done((bf16[320,512]{1,0:T(8,128)(2,1)}, bf16[320,512]{1,0:T(8,128)(2,1)S(1)}, u32[]{:S(2)}, u32[]{:S(2)}) %collective-permute-start.29) | collective-permute-done | bytes 327712 | tf_op jit(solution)/shard_map/ppermute | solution.py:32
  99.5 2.8 %collective-permute-start.23 = (bf16[3,2,64,384]{3,2,1,0:T(8,128)(2,1)S(1)}, bf16[3,2,64,384]{3,2,1,0:T(8,128)(2,1)}, u32[]{:S(2)}, u32[]{:S(2)}) collective-permute-start(bf16[3,2,64,384]{3,2,1,0:T(8,128)(2,1)S(1)} %pad_maximum_fusion.1.refs_12_), channel_id=1, source_target_pairs={{0,96},{1,97},{2,98},{3,99},{4,100},{5,101},{6,102},{7,103},{8,104... | collective-permute-start | bytes 884744 | tf_op jit(solution)/shard_map/ppermute | solution.py:32
  102.8 6.9 %collective-permute-done.23.refs_16_ = bf16[3,2,64,384]{3,2,1,0:T(8,128)(2,1)} collective-permute-done((bf16[3,2,64,384]{3,2,1,0:T(8,128)(2,1)S(1)}, bf16[3,2,64,384]{3,2,1,0:T(8,128)(2,1)}, u32[]{:S(2)}, u32[]{:S(2)}) %collective-permute-start.23) | collective-permute-done | bytes 294944 | tf_op jit(solution)/shard_map/ppermute | solution.py:32
  114.1 10.2 %collective-permute-done.22.refs_15_ = bf16[5,2,64,384]{3,2,1,0:T(8,128)(2,1)S(1)} collective-permute-done((bf16[5,2,64,384]{3,2,1,0:T(8,128)(2,1)S(1)}, bf16[5,2,64,384]{3,2,1,0:T(8,128)(2,1)S(1)}, u32[]{:S(2)}, u32[]{:S(2)}) %collective-permute-start.22) | collective-permute-done | bytes 491552 | tf_op jit(solution)/shard_map/ppermute | solution.py:32
  128.3 32.0 %shard_map.122 = (bf16[256,512]{1,0:T(8,128)(2,1)}, bf16[256,512]{1,0:T(8,128)(2,1)}, bf16[256,512]{1,0:T(8,128)(2,1)}, bf16[256,512]{1,0:T(8,128)(2,1)}, bf16[512,256]{1,0:T(8,128)(2,1)}) custom-call(s32[5]{0:T(128)} %stack.73.place, bf16[256,4096]{1,0:T(8,128)(2,1)} %shard_map.120.refs_0_, bf16[256,4096]{1,0:T(8,128)(2,1)} %copy-done.2, ...), custom_call_target="tpu_custom_call" | custom-call | tf_op jit(solution)/shard_map/pallas_call | solution.py:312
  161.5 24.6 %all_to_all.10 = bf16[256,2,256]{2,1,0:T(2,128)(2,1)S(1)} all-to-all(bf16[256,2,256]{2,1,0:T(2,128)(2,1)S(1)} %reshape.39), channel_id=1, replica_groups=mesh['fsdp'=2,'dp'=32,'owner'=4] {'owner','fsdp','dp'}, dimensions={0} | all-to-all | bytes 524288 | tf_op jit(solution)/shard_map/all_to_all | solution.py:422
  187.4 5.9 %all-to-all-start.1 = ((bf16[64,2,1024]{2,1,0:T(2,128)(2,1)}), bf16[64,2,1024]{2,1,0:T(2,128)(2,1)S(1)}, u32[]{:S(2)}, u32[]{:S(2)}) async-start(bf16[64,2,1024]{2,1,0:T(2,128)(2,1)} %broadcast_in_dim.2), calls=%async_computation.1 | async-start | bytes 524288 | tf_op jit(solution)/shard_map/all_to_all | solution.py:64
  195.3 9.5 %collective-permute-done.31.refs_2_ = bf16[256,512]{1,0:T(8,128)(2,1)S(1)} collective-permute-done((bf16[256,512]{1,0:T(8,128)(2,1)S(1)}, bf16[256,512]{1,0:T(8,128)(2,1)S(1)}, u32[]{:S(2)}, u32[]{:S(2)}) %collective-permute-start.31) | collective-permute-done | bytes 262176 | tf_op jit(solution)/shard_map/ppermute | solution.py:32
  204.8 4.8 %collective-permute-done.32.refs_3_ = bf16[256,512]{1,0:T(8,128)(2,1)S(1)} collective-permute-done((bf16[256,512]{1,0:T(8,128)(2,1)S(1)}, bf16[256,512]{1,0:T(8,128)(2,1)S(1)}, u32[]{:S(2)}, u32[]{:S(2)}) %collective-permute-start.32) | collective-permute-done | bytes 262176 | tf_op jit(solution)/shard_map/ppermute | solution.py:32
  210.3 3.4 %shard_map.123 = bf16[1,256,2048]{2,1,0:T(8,128)(2,1)} custom-call(s32[5]{0:T(128)} %stack.73.place, bf16[256,512]{1,0:T(8,128)(2,1)} %get-tuple-element.29.refs_0_, bf16[256,512]{1,0:T(8,128)(2,1)} %copy-done.20, bf16[256,512]{1,0:T(8,128)(2,1)} %copy-done.21, bf16[256,512]{1,0:T(8,128)(2,1)} %copy-done.22), custom_call_target="tpu_custom_call" | custom-call | tf_op jit(solution)/shard_map/pallas_call | solution.py:152
  (117 shorter events, 23.0 us)
Async XLA Ops:
  8.6 58.1 %collective-permute-start.1 = (bf16[256,4096]{1,0:T(8,128)(2,1)}, bf16[256,4096]{1,0:T(8,128)(2,1)}, u32[]{:S(2)}, u32[]{:S(2)}) collective-permute-start(bf16[256,4096]{1,0:T(8,128)(2,1)} %shard_map.120.refs_0_), channel_id=1, source_target_pairs={{0,2},{1,3},{2,0},{3,1},{4,6},{5,7},{6,4},{7,5},{8,10},{9,11},{10,... | collective-permute-start | bytes 6291464 | tf_op jit(solution)/shard_map/ppermute | solution.py:32
  10.1 5.8 %collective-permute-start.2 = (bf16[64,768]{1,0:T(8,128)(2,1)S(1)}, bf16[64,768]{1,0:T(8,128)(2,1)S(1)}, u32[]{:S(2)}, u32[]{:S(2)}) collective-permute-start(bf16[64,768]{1,0:T(8,128)(2,1)S(1)} %get-tuple-element.21), channel_id=1, source_target_pairs={{0,130},{1,131},{2,128},{3,129},{4,134},{5,135},{6,132},{7,133},{8... | collective-permute-start | bytes 294920 | tf_op jit(solution)/shard_map/ppermute | solution.py:32
  16.0 5.2 %collective-permute-start.5 = (bf16[2,64,384]{2,1,0:T(8,128)(2,1)S(1)}, bf16[2,64,384]{2,1,0:T(8,128)(2,1)S(1)}, u32[]{:S(2)}, u32[]{:S(2)}) collective-permute-start(bf16[2,64,384]{2,1,0:T(8,128)(2,1)S(1)} %get-tuple-element.40), channel_id=1, source_target_pairs={{0,96},{1,97},{2,98},{3,99},{4,100},{5,101},{6,102},{7,103},{8,104... | collective-permute-start | bytes 294920 | tf_op jit(solution)/shard_map/ppermute | solution.py:32
  16.7 6.1 %collective-permute-start.4 = (bf16[2,64,384]{2,1,0:T(8,128)(2,1)S(1)}, bf16[2,64,384]{2,1,0:T(8,128)(2,1)S(1)}, u32[]{:S(2)}, u32[]{:S(2)}) collective-permute-start(bf16[2,64,384]{2,1,0:T(8,128)(2,1)S(1)} %get-tuple-element.40), channel_id=1, source_target_pairs={{0,64},{1,65},{2,66},{3,67},{4,68},{5,69},{6,70},{7,71},{8,72},{9,... | collective-permute-start | bytes 294920 | tf_op jit(solution)/shard_map/ppermute | solution.py:32
  19.0 4.8 %collective-permute-start.3 = (bf16[2,64,384]{2,1,0:T(8,128)(2,1)S(1)}, bf16[2,64,384]{2,1,0:T(8,128)(2,1)S(1)}, u32[]{:S(2)}, u32[]{:S(2)}) collective-permute-start(bf16[2,64,384]{2,1,0:T(8,128)(2,1)S(1)} %get-tuple-element.40), channel_id=1, source_target_pairs={{0,32},{1,33},{2,34},{3,35},{4,36},{5,37},{6,38},{7,39},{8,40},{9,... | collective-permute-start | bytes 294920 | tf_op jit(solution)/shard_map/ppermute | solution.py:32
  23.9 11.8 %collective-permute-start.9 = (bf16[4,2,64,384]{3,2,1,0:T(8,128)(2,1)S(1)}, bf16[4,2,64,384]{3,2,1,0:T(8,128)(2,1)S(1)}, u32[]{:S(2)}, u32[]{:S(2)}) collective-permute-start(bf16[4,2,64,384]{3,2,1,0:T(8,128)(2,1)S(1)} %pad_maximum_fusion.refs_4_), channel_id=1, source_target_pairs={{0,28},{1,29},{2,30},{3,31},{4,0},{5,1},{6,2},{7,3},{8,4},{9,5},{1... | collective-permute-start | bytes 1179656 | tf_op jit(solution)/shard_map/ppermute | solution.py:32
  29.8 9.6 %collective-permute-start.6 = (bf16[4,2,64,384]{3,2,1,0:T(8,128)(2,1)S(1)}, bf16[4,2,64,384]{3,2,1,0:T(8,128)(2,1)S(1)}, u32[]{:S(2)}, u32[]{:S(2)}) collective-permute-start(bf16[4,2,64,384]{3,2,1,0:T(8,128)(2,1)S(1)} %pad_maximum_fusion.refs_4_), channel_id=1, source_target_pairs={{0,4},{1,5},{2,6},{3,7},{4,8},{5,9},{6,10},{7,11},{8,12},{9,13},{1... | collective-permute-start | bytes 1179656 | tf_op jit(solution)/shard_map/ppermute | solution.py:32
  35.7 9.5 %collective-permute-start.10 = (bf16[4,2,64,384]{3,2,1,0:T(8,128)(2,1)S(1)}, bf16[4,2,64,384]{3,2,1,0:T(8,128)(2,1)}, u32[]{:S(2)}, u32[]{:S(2)}) collective-permute-start(bf16[4,2,64,384]{3,2,1,0:T(8,128)(2,1)S(1)} %collective-permute-done.9.refs_6_), channel_id=1, source_target_pairs={{0,28},{1,29},{2,30},{3,31},{4,0},{5,1},{6,2},{7,3},{8,4},{9,5},{1... | collective-permute-start | bytes 1179656 | tf_op jit(solution)/shard_map/ppermute | solution.py:32
  39.4 9.9 %collective-permute-start.7 = (bf16[4,2,64,384]{3,2,1,0:T(8,128)(2,1)S(1)}, bf16[4,2,64,384]{3,2,1,0:T(8,128)(2,1)}, u32[]{:S(2)}, u32[]{:S(2)}) collective-permute-start(bf16[4,2,64,384]{3,2,1,0:T(8,128)(2,1)S(1)} %collective-permute-done.6.refs_5_), channel_id=1, source_target_pairs={{0,4},{1,5},{2,6},{3,7},{4,8},{5,9},{6,10},{7,11},{8,12},{9,13},{1... | collective-permute-start | bytes 1179656 | tf_op jit(solution)/shard_map/ppermute | solution.py:32
  45.2 20.8 %collective-permute-start.11 = (bf16[4,2,64,384]{3,2,1,0:T(8,128)(2,1)}, bf16[4,2,64,384]{3,2,1,0:T(8,128)(2,1)}, u32[]{:S(2)}, u32[]{:S(2)}) collective-permute-start(bf16[4,2,64,384]{3,2,1,0:T(8,128)(2,1)} %collective-permute-done.10.refs_8_), channel_id=1, source_target_pairs={{0,28},{1,29},{2,30},{3,31},{4,0},{5,1},{6,2},{7,3},{8,4},{9,5},{1... | collective-permute-start | bytes 1179656 | tf_op jit(solution)/shard_map/ppermute | solution.py:32
  49.3 17.2 %collective-permute-start.8 = (bf16[4,2,64,384]{3,2,1,0:T(8,128)(2,1)}, bf16[4,2,64,384]{3,2,1,0:T(8,128)(2,1)}, u32[]{:S(2)}, u32[]{:S(2)}) collective-permute-start(bf16[4,2,64,384]{3,2,1,0:T(8,128)(2,1)} %collective-permute-done.7.refs_7_), channel_id=1, source_target_pairs={{0,4},{1,5},{2,6},{3,7},{4,8},{5,9},{6,10},{7,11},{8,12},{9,13},{1... | collective-permute-start | bytes 1179656 | tf_op jit(solution)/shard_map/ppermute | solution.py:32
  49.3 11.3 %collective-permute-start.14 = (bf16[2,64,384]{2,1,0:T(8,128)(2,1)S(1)}, bf16[2,64,384]{2,1,0:T(8,128)(2,1)S(1)}, u32[]{:S(2)}, u32[]{:S(2)}) collective-permute-start(bf16[2,64,384]{2,1,0:T(8,128)(2,1)S(1)} %get-tuple-element.39), channel_id=1, source_target_pairs={{0,4},{1,5},{2,6},{3,7},{4,8},{5,9},{6,10},{7,11},{8,12},{9,13},{1... | collective-permute-start | bytes 294920 | tf_op jit(solution)/shard_map/ppermute | solution.py:32
  49.3 16.6 %collective-permute-start.15 = (bf16[2,64,384]{2,1,0:T(8,128)(2,1)S(1)}, bf16[2,64,384]{2,1,0:T(8,128)(2,1)}, u32[]{:S(2)}, u32[]{:S(2)}) collective-permute-start(bf16[2,64,384]{2,1,0:T(8,128)(2,1)S(1)} %get-tuple-element.39), channel_id=1, source_target_pairs={{0,28},{1,29},{2,30},{3,31},{4,0},{5,1},{6,2},{7,3},{8,4},{9,5},{1... | collective-permute-start | bytes 294920 | tf_op jit(solution)/shard_map/ppermute | solution.py:32
  60.6 9.3 %collective-permute-start.16 = (bf16[2,64,384]{2,1,0:T(8,128)(2,1)S(1)}, bf16[2,64,384]{2,1,0:T(8,128)(2,1)}, u32[]{:S(2)}, u32[]{:S(2)}) collective-permute-start(bf16[2,64,384]{2,1,0:T(8,128)(2,1)S(1)} %collective-permute-done.14), channel_id=1, source_target_pairs={{0,4},{1,5},{2,6},{3,7},{4,8},{5,9},{6,10},{7,11},{8,12},{9,13},{1... | collective-permute-start | bytes 294920 | tf_op jit(solution)/shard_map/ppermute | solution.py:32
  65.9 59.6 %collective-permute-start = (bf16[256,4096]{1,0:T(8,128)(2,1)S(1)}, bf16[256,4096]{1,0:T(8,128)(2,1)S(1)}, u32[]{:S(2)}, u32[]{:S(2)}) collective-permute-start(bf16[256,4096]{1,0:T(8,128)(2,1)S(1)} %copy-done), channel_id=1, source_target_pairs={{0,1},{1,0},{2,3},{3,2},{4,5},{5,4},{6,7},{7,6},{8,9},{9,8},{10,11... | collective-permute-start | bytes 6291464 | tf_op jit(solution)/shard_map/ppermute | solution.py:32
  66.1 23.5 %collective-permute-start.27 = (bf16[320,512]{1,0:T(8,128)(2,1)}, bf16[320,512]{1,0:T(8,128)(2,1)S(1)}, u32[]{:S(2)}, u32[]{:S(2)}) collective-permute-start(bf16[320,512]{1,0:T(8,128)(2,1)} %get-tuple-element.26), channel_id=1, source_target_pairs={{0,1},{1,0},{2,3},{3,2},{4,5},{5,4},{6,7},{7,6},{8,9},{9,8},{10,11... | collective-permute-start | bytes 983048 | tf_op jit(solution)/shard_map/ppermute | solution.py:32
  66.5 26.8 %collective-permute-start.28 = (bf16[320,512]{1,0:T(8,128)(2,1)}, bf16[320,512]{1,0:T(8,128)(2,1)S(1)}, u32[]{:S(2)}, u32[]{:S(2)}) collective-permute-start(bf16[320,512]{1,0:T(8,128)(2,1)} %get-tuple-element.27), channel_id=1, source_target_pairs={{0,2},{1,3},{2,0},{3,1},{4,6},{5,7},{6,4},{7,5},{8,10},{9,11},{10,... | collective-permute-start | bytes 983048 | tf_op jit(solution)/shard_map/ppermute | solution.py:32
  66.7 6.0 %collective-permute-start.17 = (bf16[2,64,384]{2,1,0:T(8,128)(2,1)}, bf16[2,64,384]{2,1,0:T(8,128)(2,1)S(1)}, u32[]{:S(2)}, u32[]{:S(2)}) collective-permute-start(bf16[2,64,384]{2,1,0:T(8,128)(2,1)} %collective-permute-done.15), channel_id=1, source_target_pairs={{0,28},{1,29},{2,30},{3,31},{4,0},{5,1},{6,2},{7,3},{8,4},{9,5},{1... | collective-permute-start | bytes 294920 | tf_op jit(solution)/shard_map/ppermute | solution.py:32
  69.9 57.0 %collective-permute-start.12 = (bf16[256,4096]{1,0:T(8,128)(2,1)}, bf16[256,4096]{1,0:T(8,128)(2,1)S(1)}, u32[]{:S(2)}, u32[]{:S(2)}) collective-permute-start(bf16[256,4096]{1,0:T(8,128)(2,1)} %collective-permute-done.1.refs_2_), channel_id=1, source_target_pairs={{0,1},{1,0},{2,3},{3,2},{4,5},{5,4},{6,7},{7,6},{8,9},{9,8},{10,11... | collective-permute-start | bytes 6291464 | tf_op jit(solution)/shard_map/ppermute | solution.py:32
  72.7 6.4 %collective-permute-start.18 = (bf16[2,64,384]{2,1,0:T(8,128)(2,1)}, bf16[2,64,384]{2,1,0:T(8,128)(2,1)S(1)}, u32[]{:S(2)}, u32[]{:S(2)}) collective-permute-start(bf16[2,64,384]{2,1,0:T(8,128)(2,1)} %collective-permute-done.16), channel_id=1, source_target_pairs={{0,4},{1,5},{2,6},{3,7},{4,8},{5,9},{6,10},{7,11},{8,12},{9,13},{1... | collective-permute-start | bytes 294920 | tf_op jit(solution)/shard_map/ppermute | solution.py:32
  83.7 5.8 %collective-permute-start.20 = (bf16[2,64,384]{2,1,0:T(8,128)(2,1)S(1)}, bf16[2,64,384]{2,1,0:T(8,128)(2,1)S(1)}, u32[]{:S(2)}, u32[]{:S(2)}) collective-permute-start(bf16[2,64,384]{2,1,0:T(8,128)(2,1)S(1)} %collective-permute-done.18), channel_id=1, source_target_pairs={{0,4},{1,5},{2,6},{3,7},{4,8},{5,9},{6,10},{7,11},{8,12},{9,13},{1... | collective-permute-start | bytes 294920 | tf_op jit(solution)/shard_map/ppermute | solution.py:32
  89.5 10.0 %collective-permute-start.29 = (bf16[320,512]{1,0:T(8,128)(2,1)}, bf16[320,512]{1,0:T(8,128)(2,1)S(1)}, u32[]{:S(2)}, u32[]{:S(2)}) collective-permute-start(bf16[320,512]{1,0:T(8,128)(2,1)} %get-tuple-element.28), channel_id=1, source_target_pairs={{0,3},{1,2},{2,1},{3,0},{4,7},{5,6},{6,5},{7,4},{8,11},{9,10},{10,... | collective-permute-start | bytes 983048 | tf_op jit(solution)/shard_map/ppermute | solution.py:32
  89.6 21.6 %collective-permute-start.24 = (bf16[5,2,64,384]{3,2,1,0:T(8,128)(2,1)S(1)}, bf16[5,2,64,384]{3,2,1,0:T(8,128)(2,1)S(1)}, u32[]{:S(2)}, u32[]{:S(2)}) collective-permute-start(bf16[5,2,64,384]{3,2,1,0:T(8,128)(2,1)S(1)} %bitcast_dynamic-update-slice_fusion.refs_13_), channel_id=1, source_target_pairs={{0,96},{1,97},{2,98},{3,99},{4,100},{5,101},{6,102},{7,103},{8,104... | collective-permute-start | bytes 1474568 | tf_op jit(solution)/shard_map/ppermute | solution.py:32
  93.4 9.4 %collective-permute-start.21 = (bf16[3,2,64,384]{3,2,1,0:T(8,128)(2,1)S(1)}, bf16[3,2,64,384]{3,2,1,0:T(8,128)(2,1)S(1)}, u32[]{:S(2)}, u32[]{:S(2)}) collective-permute-start(bf16[3,2,64,384]{3,2,1,0:T(8,128)(2,1)S(1)} %pad_maximum_fusion.1.refs_12_), channel_id=1, source_target_pairs={{0,32},{1,33},{2,34},{3,35},{4,36},{5,37},{6,38},{7,39},{8,40},{9,... | collective-permute-start | bytes 884744 | tf_op jit(solution)/shard_map/ppermute | solution.py:32
  99.5 10.2 %collective-permute-start.23 = (bf16[3,2,64,384]{3,2,1,0:T(8,128)(2,1)S(1)}, bf16[3,2,64,384]{3,2,1,0:T(8,128)(2,1)}, u32[]{:S(2)}, u32[]{:S(2)}) collective-permute-start(bf16[3,2,64,384]{3,2,1,0:T(8,128)(2,1)S(1)} %pad_maximum_fusion.1.refs_12_), channel_id=1, source_target_pairs={{0,96},{1,97},{2,98},{3,99},{4,100},{5,101},{6,102},{7,103},{8,104... | collective-permute-start | bytes 884744 | tf_op jit(solution)/shard_map/ppermute | solution.py:32
  102.8 9.6 %collective-permute-start.25 = (bf16[3,2,64,384]{3,2,1,0:T(8,128)(2,1)S(1)}, bf16[3,2,64,384]{3,2,1,0:T(8,128)(2,1)S(1)}, u32[]{:S(2)}, u32[]{:S(2)}) collective-permute-start(bf16[3,2,64,384]{3,2,1,0:T(8,128)(2,1)S(1)} %collective-permute-done.21.refs_14_), channel_id=1, source_target_pairs={{0,32},{1,33},{2,34},{3,35},{4,36},{5,37},{6,38},{7,39},{8,40},{9,... | collective-permute-start | bytes 884744 | tf_op jit(solution)/shard_map/ppermute | solution.py:32
  109.7 14.6 %collective-permute-start.22 = (bf16[5,2,64,384]{3,2,1,0:T(8,128)(2,1)S(1)}, bf16[5,2,64,384]{3,2,1,0:T(8,128)(2,1)S(1)}, u32[]{:S(2)}, u32[]{:S(2)}) collective-permute-start(bf16[5,2,64,384]{3,2,1,0:T(8,128)(2,1)S(1)} %bitcast_dynamic-update-slice_fusion.refs_13_), channel_id=1, source_target_pairs={{0,32},{1,33},{2,34},{3,35},{4,36},{5,37},{6,38},{7,39},{8,40},{9,... | collective-permute-start | bytes 1474568 | tf_op jit(solution)/shard_map/ppermute | solution.py:32
  111.2 13.8 %collective-permute-start.26 = (bf16[5,2,64,384]{3,2,1,0:T(8,128)(2,1)S(1)}, bf16[5,2,64,384]{3,2,1,0:T(8,128)(2,1)S(1)}, u32[]{:S(2)}, u32[]{:S(2)}) collective-permute-start(bf16[5,2,64,384]{3,2,1,0:T(8,128)(2,1)S(1)} %collective-permute-done.24.refs_17_), channel_id=1, source_target_pairs={{0,96},{1,97},{2,98},{3,99},{4,100},{5,101},{6,102},{7,103},{8,104... | collective-permute-start | bytes 1474568 | tf_op jit(solution)/shard_map/ppermute | solution.py:32
  112.5 13.0 %collective-permute-start.13 = (bf16[4,2,64,384]{3,2,1,0:T(8,128)(2,1)}, bf16[4,2,64,384]{3,2,1,0:T(8,128)(2,1)S(1)}, u32[]{:S(2)}, u32[]{:S(2)}) collective-permute-start(bf16[4,2,64,384]{3,2,1,0:T(8,128)(2,1)} %collective-permute-done.8.refs_9_), channel_id=1, source_target_pairs={{0,4},{1,5},{2,6},{3,7},{4,8},{5,9},{6,10},{7,11},{8,12},{9,13},{1... | collective-permute-start | bytes 1179656 | tf_op jit(solution)/shard_map/ppermute | solution.py:32
  187.4 26.3 %all-to-all-start.1 = ((bf16[64,2,1024]{2,1,0:T(2,128)(2,1)}), bf16[64,2,1024]{2,1,0:T(2,128)(2,1)S(1)}, u32[]{:S(2)}, u32[]{:S(2)}) async-start(bf16[64,2,1024]{2,1,0:T(2,128)(2,1)} %broadcast_in_dim.2), calls=%async_computation.1 | async-start | bytes 524288 | tf_op jit(solution)/shard_map/all_to_all | solution.py:64
  193.4 11.4 %collective-permute-start.31 = (bf16[256,512]{1,0:T(8,128)(2,1)S(1)}, bf16[256,512]{1,0:T(8,128)(2,1)S(1)}, u32[]{:S(2)}, u32[]{:S(2)}) collective-permute-start(bf16[256,512]{1,0:T(8,128)(2,1)S(1)} %copy-done.24), channel_id=1, source_target_pairs={{0,2},{1,3},{2,0},{3,1},{4,6},{5,7},{6,4},{7,5},{8,10},{9,11},{10,... | collective-permute-start | bytes 786440 | tf_op jit(solution)/shard_map/ppermute | solution.py:32
  194.0 15.6 %collective-permute-start.32 = (bf16[256,512]{1,0:T(8,128)(2,1)S(1)}, bf16[256,512]{1,0:T(8,128)(2,1)S(1)}, u32[]{:S(2)}, u32[]{:S(2)}) collective-permute-start(bf16[256,512]{1,0:T(8,128)(2,1)S(1)} %copy-done.23), channel_id=1, source_target_pairs={{0,3},{1,2},{2,1},{3,0},{4,7},{5,6},{6,5},{7,4},{8,11},{9,10},{10,... | collective-permute-start | bytes 786440 | tf_op jit(solution)/shard_map/ppermute | solution.py:32
  (28 other events, 585.1 us)
